TPU v7x, 512 devices: a whole 4x4x16 slice. The times are simulated.
512 devices in a mesh: chan: 16 (over y_hi, x, core), tm: 32 (over z, y_lo).
Axes of the slice: x: 4, y: 4 (y_hi: 2, y_lo: 2; y = y_hi * 2 + y_lo), z: 16, core: 2. Of those that a mesh axis runs over, the one named last changes fastest.
Arguments:
- ref_signal: float32 [2, 65536], P(None, 'tm'), may hold values from -40 to 40
- surveillance: float32 [2, 256, 65536], P(None, 'chan', 'tm'), may hold values from -2000 to 2000
- steering: float32 [2, 64, 256], P(None, None, 'chan'), may hold values from -0.5 to 0.5
Outputs:
- range_doppler: float32 [64, 2, 256, 256], P('chan', None, 'tm')
All inputs are finite; a program needn't handle non-finite values.
Results may differ from a plain program's by a relative error of at most 0.0003.
Values sent between devices are 32-bit elements; how exact they have to be, the bound alone decides.
A program may use at most 64 MiB of HBM per device.

v0:
```python
import math

import jax
import jax.numpy as jnp
from jax import lax
from jax.sharding import PartitionSpec as P

BEAMS = 64
LAGS = 256
DOPPLER = 256
TAPS = 64
BLOCK_LEN = 256


def from_behind(x, axis, by):
    length = lax.axis_size(axis)
    pairs = [(i, i + by) for i in range(length) if 0 <= i + by < length]
    return lax.ppermute(x, axis, pairs)


def lag_table(ref_ext, offset):
    span_len = BLOCK_LEN + LAGS + 1
    window = lax.dynamic_slice_in_dim(ref_ext, offset, span_len, 1)
    tiled_ref = jnp.tile(window, (1, LAGS))[:, : LAGS * (span_len - 1)]
    return tiled_ref.reshape(2, LAGS, span_len - 1)[:, :, LAGS : LAGS + BLOCK_LEN]


def doppler_table(first_block, block_count):
    block_ids = first_block + jnp.arange(block_count, dtype=jnp.int32)
    doppler_bins = jnp.arange(DOPPLER, dtype=jnp.int32)
    phase_arg = (block_ids[:, None] * doppler_bins[None, :] % DOPPLER).astype(jnp.float32) * (
        2.0 * math.pi / DOPPLER
    )
    cosine = jnp.cos(phase_arg)
    sine_neg = -jnp.sin(phase_arg)
    upper_rows = jnp.concatenate([cosine, sine_neg], 1)
    lower_rows = jnp.concatenate([-sine_neg, cosine], 1)
    return jnp.concatenate([upper_rows, lower_rows], 0)


def on_device(ref_signal, surveillance, steering):
    highest = lax.Precision.HIGHEST
    length = ref_signal.shape[1]
    blocks_dev = length // BLOCK_LEN
    chan_local = surveillance.shape[1]
    edge_cells = from_behind(ref_signal[:, length - LAGS :], "tm", 1)
    ref_ext = jnp.concatenate([edge_cells, ref_signal, jnp.zeros((2, 1), jnp.float32)], axis=1)
    survey = surveillance.reshape(2 * chan_local, length)
    block_ids = jnp.arange(blocks_dev, dtype=jnp.int32)

    def statistics(carry, block_idx):
        gram_sum, cross_sum = carry
        offset = block_idx * BLOCK_LEN
        basis = lag_table(ref_ext, offset)[:, :TAPS, :].reshape(2 * TAPS, BLOCK_LEN)
        portion = lax.dynamic_slice_in_dim(survey, offset, BLOCK_LEN, 1)
        gram_sum = gram_sum + jnp.dot(basis, basis.T, precision=highest)
        cross_sum = cross_sum + jnp.dot(basis, portion.T, precision=highest)
        return ((gram_sum, cross_sum), None)

    start_carry = (
        jnp.zeros((2 * TAPS, 2 * TAPS), jnp.float32),
        jnp.zeros((2 * TAPS, 2 * chan_local), jnp.float32),
    )
    (gram_sum, cross_sum), _ = lax.scan(statistics, start_carry, block_ids)
    gram_sum, cross_sum = lax.psum((gram_sum, cross_sum), "tm")
    g_real = gram_sum[:TAPS, :TAPS] + gram_sum[TAPS:, TAPS:]
    g_imag = gram_sum[:TAPS, TAPS:] - gram_sum[TAPS:, :TAPS]
    system = jnp.concatenate(
        [jnp.concatenate([g_real, -g_imag], 1), jnp.concatenate([g_imag, g_real], 1)], 0
    )
    b_real = cross_sum[:TAPS, :chan_local] + cross_sum[TAPS:, chan_local:]
    b_imag = cross_sum[:TAPS, chan_local:] - cross_sum[TAPS:, :chan_local]
    factor = jnp.linalg.cholesky(system)
    solved = jax.scipy.linalg.cho_solve((factor, True), jnp.concatenate([b_real, b_imag], 0))
    a_real = solved[:TAPS].T
    a_imag = solved[TAPS:].T
    mixing = jnp.concatenate(
        [jnp.concatenate([a_real, -a_imag], 1), jnp.concatenate([a_imag, a_real], 1)], 0
    )

    def cleanse(carry, block_idx):
        offset = block_idx * BLOCK_LEN
        basis = lag_table(ref_ext, offset)[:, :TAPS, :].reshape(2 * TAPS, BLOCK_LEN)
        portion = lax.dynamic_slice_in_dim(survey, offset, BLOCK_LEN, 1)
        return (carry, portion - jnp.dot(mixing, basis, precision=highest))

    _, cleaned_blocks = lax.scan(cleanse, None, block_ids)
    cleaned = cleaned_blocks.transpose(1, 0, 2).reshape(2 * chan_local, length)
    beams_local = BEAMS // lax.axis_size("chan")
    w_real = steering[0]
    w_imag = steering[1]
    w_rows = jnp.stack(
        [jnp.concatenate([w_real, -w_imag], 1), jnp.concatenate([w_imag, w_real], 1)], 1
    )
    w_rows = w_rows.reshape(2 * (beams_local * lax.axis_size("chan")), 2 * chan_local)
    beam_signal = lax.psum_scatter(
        jnp.dot(w_rows, cleaned, precision=highest).reshape(
            beams_local * lax.axis_size("chan"), 2, length
        ),
        "chan",
        scatter_dimension=0,
        tiled=True,
    )

    def correlate(carry, block_idx):
        offset = block_idx * BLOCK_LEN
        lag_rows = lag_table(ref_ext, offset).reshape(2 * LAGS, BLOCK_LEN)
        segment = lax.dynamic_slice_in_dim(beam_signal, offset, BLOCK_LEN, 2).reshape(
            2 * beams_local, BLOCK_LEN
        )
        product = jnp.dot(segment, lag_rows.T, precision=highest).reshape(beams_local, 2, 2, LAGS)
        real_part = product[:, 0, 0] + product[:, 1, 1]
        imag_part = product[:, 1, 0] - product[:, 0, 1]
        return (carry, jnp.stack([real_part, imag_part], 1))

    _, lagged = lax.scan(correlate, None, block_ids)
    decimated = lagged.transpose(3, 1, 2, 0)
    tm_count = lax.axis_size("tm")
    scale = 0.125 / math.sqrt(length * tm_count)
    table_local = doppler_table(lax.axis_index("tm") * blocks_dev, blocks_dev)
    portion = decimated
    flat_rows = portion.reshape(LAGS // tm_count * lax.axis_size("tm"), beams_local, 2 * blocks_dev)
    spectrum = lax.psum_scatter(
        jnp.matmul(flat_rows, table_local, precision=highest), "tm", scatter_dimension=0, tiled=True
    )
    lag_local = spectrum.shape[0]
    result = spectrum.reshape(lag_local, beams_local, 2, DOPPLER).transpose(1, 2, 0, 3) * scale
    return result


def solution(mesh):
    placed = (P(None, "tm"), P(None, "chan", "tm"), P(None, None, "chan"))
    return jax.shard_map(
        on_device,
        mesh=mesh,
        in_specs=placed,
        out_specs=P("chan", None, "tm", None),
        check_vma=False,
    )
```

profile of v0, /device:TPU:6, one launch (start us, length us, event | category | flops | bytes accessed | tf_op | source)
XLA Modules:
  0.0 707.5 jit_solution(4416383193711795709)
XLA Ops:
  6.5 0.7 slice.93
  7.2 3.5 collective-permute-start
  10.7 0.7 slice_bitcast_fusion.4
  11.4 0.7 fusion.44
  12.2 0.7 maximum_maximum_fusion.1
  12.9 37.8 %while.35 = (s32[]{:T(128)}, f32[128,128]{1,0:T(8,128)S(1)}, f32[128,32]{0,1:T(8,128)S(1)}, s32[8]{0:T(128)S(1)}, f32[2,2305]{1,0:T(2,128)S(1)}, /*index=5*/f32[...) while((s32[]{:T(128)}, f32[128,128]{1,0:T(8,128)S(1)}, ...), condition=%wide.region_1.2_spmd.clone, body=%wide.region_0.1_spmd.clone.sunk | while | flops 62955528 | bytes 8079595 | solution.py:64
  14.4 1.6 tile.40
  16.3 1.0 convolution_add_fusion.5
  17.7 0.7 dynamic_slice.58
  19.1 1.6 tile.40
  21.1 1.0 convolution_add_fusion.5
  22.4 0.7 dynamic_slice.58
  23.8 1.6 tile.40
  25.8 1.0 convolution_add_fusion.5
  28.6 1.6 tile.40
  30.5 1.0 convolution_add_fusion.5
  33.3 1.6 tile.40
  35.2 1.0 convolution_add_fusion.5
  38.0 1.6 tile.40
  40.0 1.0 convolution_add_fusion.5
  42.7 1.6 tile.40
  44.7 1.0 convolution_add_fusion.5
  47.5 1.6 tile.40
  49.4 1.0 convolution_add_fusion.5
  50.7 0.7 copy.10
  51.5 129.6 %psum.15 = f32[128,32]{0,1:T(8,128)S(1)} all-reduce(f32[128,32]{0,1:T(8,128)S(1)} %get-tuple-element.98), channel_id=1, replica_groups=mesh['chan'=16,'tm'=32] {'tm'}, use_global_device_ids=true, to_apply=%region_5.6 | all-reduce | flops 4096 | bytes 32768 | tf_op jit(solution)/shard_map/psum | solution.py:65
  181.2 129.3 %all-reduce.4.cloned.1.call-done = f32[128,128]{0,1:T(8,128)} async-done(((f32[128,128]{0,1:T(8,128)}), f32[128,128]{0,1:T(8,128)}) %all-reduce.4.cloned.1.call-update) | async-done | bytes 65552 | tf_op jit(solution)/shard_map/psum | solution.py:65
  310.5 0.9 fusion.46
  311.7 11.7 %cholesky.15 = f32[128,128]{1,0:T(8,128)S(1)} custom-call(f32[128,128]{1,0:T(8,128)S(1)} %fusion.18), custom_call_target="Cholesky" | custom-call | tf_op jit(solution)/shard_map/jit(cholesky)/cholesky | solution.py:73
  324.1 0.7 fusion.11
  324.8 9.8 %custom-call.10 = f32[1,128,128]{1,2,0:T(8,128)S(1)} custom-call(f32[1,128,128]{2,1,0:T(8,128)S(1)} %fusion.11), custom_call_target="InvertDiagBlocksLowerTriangular" | custom-call | tf_op jit(solution)/shard_map/jit(_cho_solve)/triangular_solve | solution.py:74
  335.3 34.6 %while.33 = (s32[]{:T(128)}, f32[8,32,256]{2,1,0:T(8,128)S(1)}, s32[8]{0:T(128)S(1)}, f32[32,2048]{1,0:T(8,128)}, f32[2,2305]{1,0:T(2,128)S(1)}, /*index=5*/f32[...) while((s32[]{:T(128)}, f32[8,32,256]{2,1,0:T(8,128)S(1)}, ...), condition=%wide.region_7.8_spmd, body=%wide.region_6.7_spmd.sunk | while | flops 12591112 | bytes 7833828 | solution.py:87
  336.7 1.6 tile.36
  338.6 1.0 fusion.66
  341.0 1.6 tile.36
  342.9 1.0 fusion.66
  345.3 1.6 tile.36
  347.2 1.0 fusion.66
  349.6 1.6 tile.36
  351.6 1.0 fusion.66
  354.0 1.6 tile.36
  355.9 1.0 fusion.66
  358.3 1.6 tile.36
  360.2 1.0 fusion.66
  362.6 1.6 tile.36
  364.5 1.0 fusion.66
  366.9 1.6 tile.36
  368.9 1.0 fusion.66
  370.0 2.0 fusion.19
  372.4 1.2 dynamic-slice
  374.4 144.3 %all-reduce.6.cloned.1.call-done = f32[64,2,2048]{2,0,1:T(8,128)} async-done(((f32[64,2,2048]{2,0,1:T(8,128)}), f32[64,2,2048]{2,0,1:T(8,128)}) %all-reduce.6.cloned.1.call-update) | async-done | bytes 1048592
  518.7 0.9 constant_dynamic-slice_fusion.3
  519.6 32.2 %while.34 = (s32[]{:T(128)}, f32[8,4,2,256]{3,0,2,1:T(8,128)S(1)}, s32[8]{0:T(128)S(1)}, f32[4,2,2048]{2,0,1:T(4,128)S(1)}, f32[2,2305]{1,0:T(2,128)S(1)}, /*ind...) while((s32[]{:T(128)}, f32[8,4,2,256]{3,0,2,1:T(8,128)S(1)}, s32[8]{0:T(128)S(1)}, ...), condition=%wide.region_10.11_spmd, body=%wide.region_9.10_spmd.sunk | while | flops 12587016 | bytes 7981276 | solution.py:116
  521.1 1.6 tile.38
  525.1 1.6 tile.38
  529.1 1.6 tile.38
  533.2 1.6 tile.38
  537.2 1.6 tile.38
  541.2 1.6 tile.38
  545.2 1.6 tile.38
  549.3 1.6 tile.38
  551.8 3.2 fusion.12
  555.0 144.5 %reduce-scatter.3.cloned.1.call-done = f32[8,4,512]{2,0,1:T(8,128)} async-done(((f32[256,4,512]{2,0,1:T(8,128)}), f32[8,4,512]{2,0,1:T(8,128)}) %reduce-scatter.3.cloned.1.call-update) | async-done | bytes 65552 | tf_op jit(solution)/shard_map/reduce_scatter | solution.py:123
  699.5 1.5 broadcast_multiply_fusion
  (213 shorter events, 34.1 us)
Async XLA Ops:
  6.5 304.0 %all-reduce.4.cloned.1.call-start = ((), (), s32[]{:S(2)}) async-start(), calls=%async_computation.1 | async-start | bytes 131072 | tf_op jit(solution)/shard_map/psum | solution.py:65
  7.2 4.9 collective-permute-start
  51.5 467.2 %all-reduce.6.cloned.1.call-start = ((), (), s32[]{:S(2)}) async-start(), calls=%async_computation.3 | async-start | bytes 2097152
  372.1 327.4 %reduce-scatter.3.cloned.1.call-start = ((), (), s32[]{:S(2)}) async-start(), calls=%async_computation.2 | async-start | bytes 2162688 | tf_op jit(solution)/shard_map/reduce_scatter | solution.py:123
Sparse Core Ops, SparseCore 0:
  51.6 258.8 all-reduce.3
  372.2 146.3 all-reduce.5
  555.1 144.3 reduce-scatter.2
where the time goes:
time: 709 us; the launch traced here: 708 us
  waiting for transfers between devices  418 us (59%)
  blocking collectives  130 us (18%)
  local copies, waits for them, and re-layouts  69.6 us (10%)
  matrix products  27.8 us (4%)
  other arithmetic  27.3 us (4%)
  loops' own time  17.4 us (2%)
  between operations  13.8 us (2%)
    reduce_scatter x1, waiting for transfers between devices, on_device(): lax.psum_scatter(jnp.matmul(flat_rows, table_local, precision=highest), '...  145 us
    unnamed x4, waiting for transfers between devices  144 us
    psum x1, blocking collectives, on_device(): gram_sum, cross_sum = lax.psum((gram_sum, cross_sum), 'tm')  130 us
    psum x1, waiting for transfers between devices, on_device(): gram_sum, cross_sum = lax.psum((gram_sum, cross_sum), 'tm')  129 us
    another operation x48, local copies, waits for them, and re-layouts, lag_table(): tiled_ref = jnp.tile(window, (1, LAGS))[:, :LAGS * (span_len - 1)]  40.6 us
    dynamic_slice x24, local copies, waits for them, and re-layouts, on_device(): (gram_sum, cross_sum), _ = lax.scan(statistics, start_carry, block_ids)  15.1 us
  transfers between devices with their start and end apart: 4, of which 3 were waited for; matrix products, arithmetic and copies ran while one was open for 0% of the time, Pallas kernels for 0%

commit v1 on v0

v1 whole, which is shorter than its diff:
```python
import functools
import math

import jax
import jax.numpy as jnp
import numpy as np
from jax import lax
from jax.experimental import pallas as pl
from jax.experimental.pallas import tpu as pltpu
from jax.sharding import PartitionSpec as P

LAGS = 256
DOPPLER = 256
TAPS = 64
BLOCK = 256
HALO = 256
MESH = pl.DeviceIdType.MESH
HIGHEST = lax.Precision.HIGHEST


def dot(a, b):
    return lax.dot_general(a, b, (((1,), (0,)), ((), ())), precision=HIGHEST, preferred_element_type=jnp.float32)


def dot_nt(a, b):
    return lax.dot_general(a, b, (((1,), (1,)), ((), ())), precision=HIGHEST, preferred_element_type=jnp.float32)


def iota(shape, dim):
    return lax.broadcasted_iota(jnp.int32, shape, dim)


def conj_pack(a, b):
    half = a.shape[1] // 2
    sign = jnp.where(iota(a.shape, 1) < half, 1.0, -1.0)
    return sign * a + pltpu.roll(b, half, 1)


def widen(packed):
    half = packed.shape[1] // 2
    sign = jnp.where(iota(packed.shape, 1) < half, 1.0, -1.0)
    return jnp.concatenate([packed * sign, pltpu.roll(packed, half, 1)], 0)


def hermitian_inverse(m):
    n = m.shape[0]
    lane = iota((1, 2 * n), 1)
    row_id = iota((n, 1), 0)
    for k in range(n):
        col_re = m[:, k : k + 1]
        col_im = m[:, n + k : n + k + 1]
        row = m[k : k + 1, :]
        inv = 1.0 / m[k : k + 1, k : k + 1]
        here = (lane == k) | (lane == n + k)
        row = jnp.where(here, jnp.where(lane == k, 1.0, 0.0), row) * inv
        turned = pltpu.roll(row, n, 1) * jnp.where(lane < n, -1.0, 1.0)
        rest = jnp.where(here, 0.0, m) - col_re * row - col_im * turned
        m = jnp.where(row_id == k, row, rest)
    return m


def gram_matrix(g_row, e_row):
    n = TAPS
    row = iota((n, 2 * n), 0)
    lane = iota((n, 2 * n), 1)
    col = lane % n
    sign = jnp.where(lane < n, 1.0, -1.0)

    def shifted(v):
        return pltpu.roll(jnp.broadcast_to(v, (n, 2 * n)), 0, 1, stride=1, stride_axis=0)

    upper = jnp.where(col >= row, shifted(g_row), 0.0)
    flipped = jnp.concatenate([upper, jnp.zeros_like(upper)], 0).T
    lower = flipped[:n] - pltpu.roll(flipped[n:], n, 1)
    toeplitz = jnp.where(col >= row, upper, lower)
    tail = jnp.where((col >= row) & (row >= 1), shifted(e_row), 0.0)
    tail = jnp.concatenate([tail, jnp.zeros_like(tail)], 0)
    square = dot(tail.T, tail)
    return toeplitz - (square[:n] + sign * pltpu.roll(square[n:], n, 1))


def kernel(nc, nt, ref_ref, surv_ref, w_ref, table_ref, out_ref,
           part, rs_buf, halo, lagt, gm, gm_buf, xm, xm_buf, emb, lg, lg_buf,
           halo_ss, halo_rs, rs_ss, rs_rs, gm_ss, gm_rs, xm_ss, xm_rs, lg_ss, lg_rs):
    c = lax.axis_index("chan")
    d = lax.axis_index("tm")
    length = ref_ref.shape[1]
    beams = part.shape[1] // 2
    blocks = length // BLOCK

    def tm_peer(j):
        return lax.rem(d + nt // 2 + (1 - 2 * (j % 2)) * ((j + 1) // 2) + nt, nt)

    def chan_peer(j):
        return lax.rem(c + 1 + j, nc)

    barrier = pltpu.get_barrier_semaphore()

    def greet_chan(j, _):
        pl.semaphore_signal(barrier, inc=1, device_id={"chan": chan_peer(j)}, device_id_type=MESH)
        return 0

    def greet_tm(j, _):
        pl.semaphore_signal(barrier, inc=1, device_id={"tm": tm_peer(j)}, device_id_type=MESH)
        return 0

    lax.fori_loop(0, nt - 1, greet_tm, 0)
    lax.fori_loop(0, nc - 1, greet_chan, 0)

    partial = dot(w_ref[...], surv_ref[...])
    for dest in range(nc):
        part[dest] = partial[2 * beams * dest : 2 * beams * (dest + 1), :]

    pl.semaphore_wait(barrier, nt - 1 + nc - 1)

    right = lax.rem(d + 1, nt)
    halo_copy = pltpu.make_async_remote_copy(
        src_ref=ref_ref.at[:, pl.ds(length - HALO, HALO)], dst_ref=halo, send_sem=halo_ss, recv_sem=halo_rs,
        device_id={"tm": right}, device_id_type=MESH)
    halo_copy.start()

    def rs_copy(peer, slot):
        return pltpu.make_async_remote_copy(
            src_ref=part.at[peer], dst_ref=rs_buf.at[slot], send_sem=rs_ss.at[peer], recv_sem=rs_rs.at[slot],
            device_id={"chan": peer}, device_id_type=MESH)

    def rs_start(j, _):
        rs_copy(chan_peer(j), c).start()
        return 0

    lax.fori_loop(0, nc - 1, rs_start, 0)

    halo_copy.wait()
    ref = ref_ref[...]
    before = jnp.where(d == 0, 0.0, halo[...])
    extended = jnp.concatenate([before, ref], 1)
    for p in range(2):
        shifted = pltpu.roll(
            jnp.broadcast_to(extended[p : p + 1, :], (LAGS, HALO + length)), 0, 1, stride=1, stride_axis=0)
        lagt[p] = shifted[:, HALO:]
    taps = jnp.concatenate([lagt[0, :TAPS, :], lagt[1, :TAPS, :]], 0)

    row8 = iota((8, length), 0)
    mark = jnp.where((iota((8, length), 1) == length - 1) & (d == nt - 1), 1.0, 0.0)
    probe = jnp.where(row8 == 0, ref[0:1], jnp.where(row8 == 1, ref[1:2], jnp.where(row8 == 2, mark, 0.0)))
    g_raw = dot_nt(probe, taps)
    g_conj = conj_pack(g_raw[0:1], g_raw[1:2])
    gm[0:1, :] = jnp.where(iota(g_conj.shape, 1) < TAPS, g_conj, -g_conj)
    gm[1:2, :] = g_raw[2:3]

    def gm_copy(peer, slot):
        return pltpu.make_async_remote_copy(
            src_ref=gm, dst_ref=gm_buf.at[slot], send_sem=gm_ss.at[peer], recv_sem=gm_rs.at[slot],
            device_id={"tm": peer}, device_id_type=MESH)

    def xm_copy(peer, slot):
        return pltpu.make_async_remote_copy(
            src_ref=xm, dst_ref=xm_buf.at[slot], send_sem=xm_ss.at[peer], recv_sem=xm_rs.at[slot],
            device_id={"tm": peer}, device_id_type=MESH)

    def lg_copy(peer, slot):
        return pltpu.make_async_remote_copy(
            src_ref=lg.at[peer], dst_ref=lg_buf.at[slot], send_sem=lg_ss.at[peer], recv_sem=lg_rs.at[slot],
            device_id={"tm": peer}, device_id_type=MESH)

    def tm_start(copy):
        def body(j, _):
            copy(tm_peer(j), d).start()
            return 0

        lax.fori_loop(0, nt - 1, body, 0)

    def tm_wait_recv(copy):
        def body(j, _):
            peer = tm_peer(j)
            copy(peer, peer).wait_recv()
            return 0

        lax.fori_loop(0, nt - 1, body, 0)

    def tm_wait_send(copy):
        def body(j, _):
            peer = tm_peer(j)
            copy(peer, peer).wait_send()
            return 0

        lax.fori_loop(0, nt - 1, body, 0)

    tm_start(gm_copy)
    gm_buf[d] = gm[...]

    def rs_wait(j, _):
        peer = chan_peer(j)
        rs_copy(peer, peer).wait_recv()
        return 0

    lax.fori_loop(0, nc - 1, rs_wait, 0)
    rs_buf[c] = part[c]
    total = rs_buf[0]
    for source in range(1, nc):
        total = total + rs_buf[source]

    x_raw = dot_nt(total, taps)
    xm[...] = conj_pack(x_raw[:beams], x_raw[beams:])
    tm_start(xm_copy)
    xm_buf[d] = xm[...]

    tm_wait_recv(gm_copy)
    g_sum = jnp.sum(gm_buf[...], axis=0)
    gram = gram_matrix(g_sum[0:1], g_sum[1:2])
    inverse = widen(hermitian_inverse(gram))
    gram_wide = widen(gram)

    tm_wait_recv(xm_copy)
    x = jnp.sum(xm_buf[...], axis=0)
    weights = dot(x, inverse)
    weights = weights + dot(x - dot(weights, gram_wide), inverse)

    sign = jnp.where(iota(weights.shape, 1) < TAPS, 1.0, -1.0)
    both = jnp.concatenate([weights * sign, pltpu.roll(weights, TAPS, 1)], 0)
    clean = total - dot(both, taps)

    inside = iota((blocks, length), 1) // BLOCK == iota((blocks, length), 0)

    def spread(row):
        return jnp.where(inside, jnp.broadcast_to(row, (blocks, length)), 0.0)

    for m in range(beams):
        re, im = clean[m : m + 1], clean[beams + m : beams + m + 1]
        base = 2 * blocks * m
        emb[0, base : base + blocks, :] = spread(re)
        emb[0, base + blocks : base + 2 * blocks, :] = spread(im)
        emb[1, base : base + blocks, :] = spread(im)
        emb[1, base + blocks : base + 2 * blocks, :] = spread(-re)
    lagged = dot_nt(lagt[0], emb[0]) + dot_nt(lagt[1], emb[1])
    own = LAGS // nt
    for dest in range(nt):
        lg[dest] = lagged[own * dest : own * (dest + 1), :]
    tm_start(lg_copy)
    lg_buf[d] = lg[d]
    tm_wait_recv(lg_copy)

    wide = 2 * blocks
    group = 128 // wide
    slot_of = iota((own, 128), 1) // wide
    rows = []
    for m in range(beams):
        pieces = []
        for start in range(0, nt, group):
            acc = jnp.zeros((own, 128), jnp.float32)
            for s in range(group):
                moved = pltpu.roll(lg_buf[start + s], (wide * (s - m)) % 128, 1)
                acc = jnp.where(slot_of == s, moved, acc)
            pieces.append(acc)
        rows.append(jnp.concatenate(pieces, 1))
    spectrum = dot(jnp.concatenate(rows, 0), table_ref[...])
    for m in range(beams):
        for part_id in range(2):
            out_ref[m, part_id] = spectrum[own * m : own * (m + 1), DOPPLER * part_id : DOPPLER * (part_id + 1)]

    tm_wait_send(gm_copy)
    tm_wait_send(xm_copy)
    tm_wait_send(lg_copy)

    def rs_drain(j, _):
        peer = chan_peer(j)
        rs_copy(peer, peer).wait_send()
        return 0

    lax.fori_loop(0, nc - 1, rs_drain, 0)


def doppler_table(blocks_total, blocks):
    q = np.arange(blocks_total)
    angle = 2.0 * np.pi * ((q[:, None] * np.arange(DOPPLER)[None, :]) % DOPPLER) / DOPPLER
    cosine, sine = np.cos(angle), np.sin(angle)
    first = np.concatenate([cosine, -sine], 1).reshape(-1, 1, blocks, 2 * DOPPLER)
    second = np.concatenate([sine, cosine], 1).reshape(-1, 1, blocks, 2 * DOPPLER)
    scale = 0.125 / math.sqrt(blocks_total * BLOCK)
    table = np.concatenate([first, second], 1).reshape(2 * blocks_total, 2 * DOPPLER) * scale
    return table.astype(np.float32)


def on_device(ref_signal, surveillance, steering):
    nc, nt = lax.axis_size("chan"), lax.axis_size("tm")
    length = ref_signal.shape[1]
    chans = surveillance.shape[1]
    beams = steering.shape[1] // nc
    blocks = length // BLOCK
    own = LAGS // nt
    w = steering.reshape(2, nc, beams, chans)
    rows = jnp.stack([jnp.concatenate([w[0], -w[1]], -1), jnp.concatenate([w[1], w[0]], -1)], 1)
    table = jnp.asarray(doppler_table(nt * blocks, blocks))
    vmem = pl.BlockSpec(memory_space=pltpu.VMEM)
    f32 = jnp.float32
    cols = 2 * blocks * beams
    return pl.pallas_call(
        functools.partial(kernel, nc, nt),
        out_shape=jax.ShapeDtypeStruct((beams, 2, own, DOPPLER), f32),
        in_specs=[vmem] * 4,
        out_specs=vmem,
        scratch_shapes=[
            pltpu.VMEM((nc, 2 * beams, length), f32),
            pltpu.VMEM((nc, 2 * beams, length), f32),
            pltpu.VMEM((2, HALO), f32),
            pltpu.VMEM((2, LAGS, length), f32),
            pltpu.VMEM((2, 2 * TAPS), f32),
            pltpu.VMEM((nt, 2, 2 * TAPS), f32),
            pltpu.VMEM((beams, 2 * TAPS), f32),
            pltpu.VMEM((nt, beams, 2 * TAPS), f32),
            pltpu.VMEM((2, 128, length), f32),
            pltpu.VMEM((nt, own, 128), f32),
            pltpu.VMEM((nt, own, 128), f32),
            pltpu.SemaphoreType.DMA,
            pltpu.SemaphoreType.DMA,
            pltpu.SemaphoreType.DMA((nc,)),
            pltpu.SemaphoreType.DMA((nc,)),
            pltpu.SemaphoreType.DMA((nt,)),
            pltpu.SemaphoreType.DMA((nt,)),
            pltpu.SemaphoreType.DMA((nt,)),
            pltpu.SemaphoreType.DMA((nt,)),
            pltpu.SemaphoreType.DMA((nt,)),
            pltpu.SemaphoreType.DMA((nt,)),
        ],
        compiler_params=pltpu.CompilerParams(collective_id=0, has_side_effects=True, vmem_limit_bytes=60 << 20),
        name="radar",
    )(ref_signal, surveillance.reshape(2 * chans, length), rows.reshape(2 * beams * nc, 2 * chans), table)


def solution(mesh):
    placed = (P(None, "tm"), P(None, "chan", "tm"), P(None, None, "chan"))
    return jax.shard_map(
        on_device,
        mesh=mesh,
        in_specs=placed,
        out_specs=P("chan", None, "tm", None),
        check_vma=False,
    )
```

time: 709 us -> 70.7 us (0.10)
  the two profiles are of different devices: /device:TPU:6 before, /device:TPU:10 now
where the time goes in v1:
time: 70.7 us; the launch traced here: 70.5 us
  Pallas kernels  67.3 us (95%)
  local copies, waits for them, and re-layouts  3 us (4%)
    pallas_call x1, Pallas kernels, on_device(): pl.pallas_call(functools.partial(kernel, nc, nt), out_shape=jax.ShapeDtyp...  67.3 us
    unnamed x3, local copies, waits for them, and re-layouts  1.64 us

profile of v1, /device:TPU:10, one launch (start us, length us, event | category | flops | bytes accessed | tf_op | source)
XLA Modules:
  0.0 70.5 jit_solution(5344886601411642439)
XLA Ops:
  0.0 0.7 %fusion = (f32[1,64,16]{1,2,0:T(8,128)S(1)}, f32[1,64,16]{1,2,0:T(8,128)S(1)}) fusion(f32[2,64,16]{1,2,0:T(8,128)} %param.6), kind=kLoop, calls=%fused_computation.3 | loop fusion | bytes 16384 | tf_op jit(solution)/shard_map/slice | solution.py:292
  0.7 0.1 copy.13
  0.8 0.1 copy.12
  0.9 0.1 maximum_bitcast_fusion
  1.0 0.6 copy.11
  1.7 67.3 %radar.1 = f32[4,2,8,256]{3,2,1,0:T(8,128)} custom-call(f32[2,2048]{1,0:T(2,128)} %ref_ref.1, f32[32,2048]{1,0:T(8,128)} %bitcast.11, f32[128,32]{1,0:T(8,128)} %bitcast.10, f32[512,512]{1,0:T(8,128)} %constant.2.clone.table_ref), custom_call_target="tpu_custom_call" | custom-call | tf_op jit(solution)/shard_map/radar/pallas_call | solution.py:297
  69.0 1.5 %copy.15 = f32[4,2,8,256]{3,2,1,0:T(8,128)} copy(f32[4,2,8,256]{3,2,1,0:T(8,128)} %radar.1) | data formatting | bytes 131072
  (2 shorter events, 0.0 us)

commit v2 on v1

--- a/solution.py
+++ b/solution.py
@@ -26,6 +26,23 @@
     return lax.dot_general(a, b, (((1,), (1,)), ((), ())), precision=HIGHEST, preferred_element_type=jnp.float32)
 
 
+def bdot(a, b):
+    return lax.dot_general(a, b, (((1,), (0,)), ((), ())), preferred_element_type=jnp.float32)
+
+
+def bdot_nt(a, b):
+    return lax.dot_general(a, b, (((1,), (1,)), ((), ())), preferred_element_type=jnp.float32)
+
+
+def split(x, terms):
+    out = []
+    for _ in range(terms):
+        head = x.astype(jnp.bfloat16).astype(jnp.float32)
+        out.append(head)
+        x = x - head
+    return out
+
+
 def iota(shape, dim):
     return lax.broadcasted_iota(jnp.int32, shape, dim)
 
@@ -44,18 +61,28 @@
 
 def hermitian_inverse(m):
     n = m.shape[0]
+    wide = (n, 2 * n)
     lane = iota((1, 2 * n), 1)
     row_id = iota((n, 1), 0)
-    for k in range(n):
-        col_re = m[:, k : k + 1]
-        col_im = m[:, n + k : n + k + 1]
-        row = m[k : k + 1, :]
-        inv = 1.0 / m[k : k + 1, k : k + 1]
-        here = (lane == k) | (lane == n + k)
-        row = jnp.where(here, jnp.where(lane == k, 1.0, 0.0), row) * inv
-        turned = pltpu.roll(row, n, 1) * jnp.where(lane < n, -1.0, 1.0)
-        rest = jnp.where(here, 0.0, m) - col_re * row - col_im * turned
-        m = jnp.where(row_id == k, row, rest)
+    flip = jnp.where(lane < n, -1.0, 1.0)
+    for k in range(0, n, 2):
+        c0r, c1r, c0i, c1i = (jnp.broadcast_to(m[:, j : j + 1], wide) for j in (k, k + 1, n + k, n + k + 1))
+        a, d = c0r[k : k + 1], c1r[k + 1 : k + 2]
+        br, bi = c1r[k : k + 1], c1i[k : k + 1]
+        inv = 1.0 / (a * d - (br * br + bi * bi))
+        at0, at1 = lane == k, lane == k + 1
+        here = at0 | at1 | (lane == n + k) | (lane == n + k + 1)
+        r0 = jnp.where(here, jnp.where(at0, 1.0, 0.0), m[k : k + 1])
+        r1 = jnp.where(here, jnp.where(at1, 1.0, 0.0), m[k + 1 : k + 2])
+        t0 = pltpu.roll(r0, n, 1) * flip
+        t1 = pltpu.roll(r1, n, 1) * flip
+        a, d, br, bi = a * inv, d * inv, br * inv, bi * inv
+        n0 = d * r0 - br * r1 - bi * t1
+        u0 = d * t0 - br * t1 + bi * r1
+        n1 = a * r1 - br * r0 + bi * t0
+        u1 = a * t1 - br * t0 - bi * r0
+        rest = (jnp.where(here, 0.0, m) - c0r * n0 - c1r * n1) - (c0i * u0 + c1i * u1)
+        m = jnp.where(row_id == k, n0, jnp.where(row_id == k + 1, n1, rest))
     return m
 
 
@@ -80,12 +107,15 @@
 
 
 def kernel(nc, nt, ref_ref, surv_ref, w_ref, table_ref, out_ref,
-           part, rs_buf, halo, lagt, gm, gm_buf, xm, xm_buf, emb, lg, lg_buf,
-           halo_ss, halo_rs, rs_ss, rs_rs, gm_ss, gm_rs, xm_ss, xm_rs, lg_ss, lg_rs):
+           part, core_buf, chip_send, chip_buf, halo, lagt, lag_hi, lag_mid, tap_lo, gm, gm_buf, xm, xm_buf, emb, lg, lg_buf,
+           halo_ss, halo_rs, core_ss, core_rs, rs_ss, rs_rs, gm_ss, gm_rs, xm_ss, xm_rs, lg_ss, lg_rs):
     c = lax.axis_index("chan")
     d = lax.axis_index("tm")
     length = ref_ref.shape[1]
-    beams = part.shape[1] // 2
+    beams = part.shape[2] // 2
+    chips = nc // 2
+    core, chip = c % 2, c // 2
+    partner = c + 1 - 2 * core
     blocks = length // BLOCK
 
     def tm_peer(j):
@@ -107,9 +137,13 @@
     lax.fori_loop(0, nt - 1, greet_tm, 0)
     lax.fori_loop(0, nc - 1, greet_chan, 0)
 
-    partial = dot(w_ref[...], surv_ref[...])
-    for dest in range(nc):
-        part[dest] = partial[2 * beams * dest : 2 * beams * (dest + 1), :]
+    w_re, w_im = w_ref[0], w_ref[1]
+    survey = jnp.concatenate([surv_ref[0], surv_ref[1]], 0)
+    part_re = dot(jnp.concatenate([w_re, -w_im], 1), survey)
+    part_im = dot(jnp.concatenate([w_im, w_re], 1), survey)
+    for owner in range(nc):
+        rows = slice(beams * owner, beams * (owner + 1))
+        part[owner % 2, owner // 2] = jnp.concatenate([part_re[rows], part_im[rows]], 0)
 
     pl.semaphore_wait(barrier, nt - 1 + nc - 1)
 
@@ -119,16 +153,35 @@
         device_id={"tm": right}, device_id_type=MESH)
     halo_copy.start()
 
+    def chip_peer(j):
+        return lax.rem(chip + 1 + j, chips)
+
+    def core_copy(j):
+        return pltpu.make_async_remote_copy(
+            src_ref=part.at[1 - core, j], dst_ref=core_buf.at[j], send_sem=core_ss.at[j], recv_sem=core_rs.at[j],
+            device_id={"chan": partner}, device_id_type=MESH)
+
     def rs_copy(peer, slot):
         return pltpu.make_async_remote_copy(
-            src_ref=part.at[peer], dst_ref=rs_buf.at[slot], send_sem=rs_ss.at[peer], recv_sem=rs_rs.at[slot],
-            device_id={"chan": peer}, device_id_type=MESH)
+            src_ref=chip_send.at[peer], dst_ref=chip_buf.at[slot], send_sem=rs_ss.at[peer], recv_sem=rs_rs.at[slot],
+            device_id={"chan": 2 * peer + core}, device_id_type=MESH)
+
+    def core_start(j, _):
+        core_copy(chip_peer(j)).start()
+        return 0
+
+    lax.fori_loop(0, chips, core_start, 0)
 
     def rs_start(j, _):
-        rs_copy(chan_peer(j), c).start()
-        return 0
-
-    lax.fori_loop(0, nc - 1, rs_start, 0)
+        peer = chip_peer(j)
+        core_copy(peer).wait_recv()
+        chip_send[peer] = part[core, peer] + core_buf[peer]
+        rs_copy(peer, chip).start()
+        return 0
+
+    lax.fori_loop(0, chips - 1, rs_start, 0)
+    core_copy(chip).wait_recv()
+    chip_buf[chip] = part[core, chip] + core_buf[chip]
 
     halo_copy.wait()
     ref = ref_ref[...]
@@ -189,18 +242,28 @@
     tm_start(gm_copy)
     gm_buf[d] = gm[...]
 
+    for p in range(2):
+        hi, mid, lo = split(lagt[p], 3)
+        lag_hi[LAGS * p : LAGS * (p + 1)] = hi.astype(jnp.bfloat16)
+        lag_mid[LAGS * p : LAGS * (p + 1)] = mid.astype(jnp.bfloat16)
+        tap_lo[TAPS * p : TAPS * (p + 1)] = lo[:TAPS].astype(jnp.bfloat16)
+    tap_terms = [jnp.concatenate([lag_hi[:TAPS], lag_hi[LAGS : LAGS + TAPS]], 0),
+                 jnp.concatenate([lag_mid[:TAPS], lag_mid[LAGS : LAGS + TAPS]], 0), tap_lo[...]]
+
     def rs_wait(j, _):
-        peer = chan_peer(j)
+        peer = chip_peer(j)
         rs_copy(peer, peer).wait_recv()
         return 0
 
-    lax.fori_loop(0, nc - 1, rs_wait, 0)
-    rs_buf[c] = part[c]
-    total = rs_buf[0]
-    for source in range(1, nc):
-        total = total + rs_buf[source]
-
-    x_raw = dot_nt(total, taps)
+    lax.fori_loop(0, chips - 1, rs_wait, 0)
+    total = chip_buf[0]
+    for source in range(1, chips):
+        total = total + chip_buf[source]
+
+    total_terms = jnp.concatenate(split(total, 3), 0).astype(jnp.bfloat16)
+    x_cols = sum(bdot_nt(term, total_terms) for term in tap_terms)
+    x_rows = jnp.concatenate([x_cols, jnp.zeros((2 * TAPS, 128 - x_cols.shape[1]), jnp.float32)], 1).T
+    x_raw = x_rows[: 2 * beams] + x_rows[2 * beams : 4 * beams] + x_rows[4 * beams : 6 * beams]
     xm[...] = conj_pack(x_raw[:beams], x_raw[beams:])
     tm_start(xm_copy)
     xm_buf[d] = xm[...]
@@ -208,31 +271,39 @@
     tm_wait_recv(gm_copy)
     g_sum = jnp.sum(gm_buf[...], axis=0)
     gram = gram_matrix(g_sum[0:1], g_sum[1:2])
+    level = 1.0 / gram[0:1, 0:1]
+    gram = gram * level
     inverse = widen(hermitian_inverse(gram))
     gram_wide = widen(gram)
 
     tm_wait_recv(xm_copy)
-    x = jnp.sum(xm_buf[...], axis=0)
+    x = jnp.sum(xm_buf[...], axis=0) * level
     weights = dot(x, inverse)
     weights = weights + dot(x - dot(weights, gram_wide), inverse)
 
     sign = jnp.where(iota(weights.shape, 1) < TAPS, 1.0, -1.0)
     both = jnp.concatenate([weights * sign, pltpu.roll(weights, TAPS, 1)], 0)
-    clean = total - dot(both, taps)
+    both_terms = jnp.concatenate(split(both, 3), 0).astype(jnp.bfloat16)
+    model = sum(bdot(both_terms, term) for term in tap_terms)
+    clean = total - (model[: 2 * beams] + model[2 * beams : 4 * beams] + model[4 * beams : 6 * beams])
 
     inside = iota((blocks, length), 1) // BLOCK == iota((blocks, length), 0)
+    cols = 2 * blocks * beams
 
     def spread(row):
         return jnp.where(inside, jnp.broadcast_to(row, (blocks, length)), 0.0)
 
-    for m in range(beams):
-        re, im = clean[m : m + 1], clean[beams + m : beams + m + 1]
-        base = 2 * blocks * m
-        emb[0, base : base + blocks, :] = spread(re)
-        emb[0, base + blocks : base + 2 * blocks, :] = spread(im)
-        emb[1, base : base + blocks, :] = spread(im)
-        emb[1, base + blocks : base + 2 * blocks, :] = spread(-re)
-    lagged = dot_nt(lagt[0], emb[0]) + dot_nt(lagt[1], emb[1])
+    for order, term in enumerate(split(clean, 2)):
+        for m in range(beams):
+            base = cols * order + 2 * blocks * m
+            pair = jnp.concatenate([spread(term[m : m + 1]), spread(term[beams + m : beams + m + 1])], 0)
+            emb[base : base + 2 * blocks, :] = pair.astype(jnp.bfloat16)
+    products = bdot_nt(lag_hi[...], emb[...]) + bdot_nt(lag_mid[...], emb[...])
+    products = products + pltpu.roll(products, cols, 1)
+    with_re, with_im = products[:LAGS], products[LAGS:]
+    real_lane = iota((LAGS, 2 * cols), 1) % (2 * blocks) < blocks
+    lagged = with_re + jnp.where(
+        real_lane, pltpu.roll(with_im, 2 * cols - blocks, 1), -pltpu.roll(with_im, blocks, 1))
     own = LAGS // nt
     for dest in range(nt):
         lg[dest] = lagged[own * dest : own * (dest + 1), :]
@@ -253,7 +324,11 @@
                 acc = jnp.where(slot_of == s, moved, acc)
             pieces.append(acc)
         rows.append(jnp.concatenate(pieces, 1))
-    spectrum = dot(jnp.concatenate(rows, 0), table_ref[...])
+    stacked = jnp.concatenate(rows, 0)
+    height = own * beams
+    stacked_terms = jnp.concatenate(split(stacked, 2), 0).astype(jnp.bfloat16)
+    spectrum = bdot(stacked_terms, table_ref[0]) + bdot(stacked_terms, table_ref[1])
+    spectrum = spectrum[:height] + spectrum[height:]
     for m in range(beams):
         for part_id in range(2):
             out_ref[m, part_id] = spectrum[own * m : own * (m + 1), DOPPLER * part_id : DOPPLER * (part_id + 1)]
@@ -263,11 +338,16 @@
     tm_wait_send(lg_copy)
 
     def rs_drain(j, _):
-        peer = chan_peer(j)
+        peer = chip_peer(j)
         rs_copy(peer, peer).wait_send()
         return 0
 
-    lax.fori_loop(0, nc - 1, rs_drain, 0)
+    def core_drain(j, _):
+        core_copy(j).wait_send()
+        return 0
+
+    lax.fori_loop(0, chips - 1, rs_drain, 0)
+    lax.fori_loop(0, chips, core_drain, 0)
 
 
 def doppler_table(blocks_total, blocks):
@@ -278,7 +358,9 @@
     second = np.concatenate([sine, cosine], 1).reshape(-1, 1, blocks, 2 * DOPPLER)
     scale = 0.125 / math.sqrt(blocks_total * BLOCK)
     table = np.concatenate([first, second], 1).reshape(2 * blocks_total, 2 * DOPPLER) * scale
-    return table.astype(np.float32)
+    head = table.astype(np.float32).astype(jnp.bfloat16)
+    tail = (table - head.astype(np.float64)).astype(np.float32).astype(jnp.bfloat16)
+    return np.stack([head, tail])
 
 
 def on_device(ref_signal, surveillance, steering):
@@ -288,33 +370,38 @@
     beams = steering.shape[1] // nc
     blocks = length // BLOCK
     own = LAGS // nt
-    w = steering.reshape(2, nc, beams, chans)
-    rows = jnp.stack([jnp.concatenate([w[0], -w[1]], -1), jnp.concatenate([w[1], w[0]], -1)], 1)
     table = jnp.asarray(doppler_table(nt * blocks, blocks))
     vmem = pl.BlockSpec(memory_space=pltpu.VMEM)
-    f32 = jnp.float32
-    cols = 2 * blocks * beams
+    f32, bf16 = jnp.float32, jnp.bfloat16
+    chips = nc // 2
     return pl.pallas_call(
         functools.partial(kernel, nc, nt),
         out_shape=jax.ShapeDtypeStruct((beams, 2, own, DOPPLER), f32),
         in_specs=[vmem] * 4,
         out_specs=vmem,
         scratch_shapes=[
-            pltpu.VMEM((nc, 2 * beams, length), f32),
-            pltpu.VMEM((nc, 2 * beams, length), f32),
+            pltpu.VMEM((2, chips, 2 * beams, length), f32),
+            pltpu.VMEM((chips, 2 * beams, length), f32),
+            pltpu.VMEM((chips, 2 * beams, length), f32),
+            pltpu.VMEM((chips, 2 * beams, length), f32),
             pltpu.VMEM((2, HALO), f32),
             pltpu.VMEM((2, LAGS, length), f32),
+            pltpu.VMEM((2 * LAGS, length), bf16),
+            pltpu.VMEM((2 * LAGS, length), bf16),
+            pltpu.VMEM((2 * TAPS, length), bf16),
             pltpu.VMEM((2, 2 * TAPS), f32),
             pltpu.VMEM((nt, 2, 2 * TAPS), f32),
             pltpu.VMEM((beams, 2 * TAPS), f32),
             pltpu.VMEM((nt, beams, 2 * TAPS), f32),
-            pltpu.VMEM((2, 128, length), f32),
+            pltpu.VMEM((4 * blocks * beams, length), bf16),
             pltpu.VMEM((nt, own, 128), f32),
             pltpu.VMEM((nt, own, 128), f32),
             pltpu.SemaphoreType.DMA,
             pltpu.SemaphoreType.DMA,
-            pltpu.SemaphoreType.DMA((nc,)),
-            pltpu.SemaphoreType.DMA((nc,)),
+            pltpu.SemaphoreType.DMA((chips,)),
+            pltpu.SemaphoreType.DMA((chips,)),
+            pltpu.SemaphoreType.DMA((chips,)),
+            pltpu.SemaphoreType.DMA((chips,)),
             pltpu.SemaphoreType.DMA((nt,)),
             pltpu.SemaphoreType.DMA((nt,)),
             pltpu.SemaphoreType.DMA((nt,)),
@@ -324,7 +411,7 @@
         ],
         compiler_params=pltpu.CompilerParams(collective_id=0, has_side_effects=True, vmem_limit_bytes=60 << 20),
         name="radar",
-    )(ref_signal, surveillance.reshape(2 * chans, length), rows.reshape(2 * beams * nc, 2 * chans), table)
+    )(ref_signal, surveillance, steering, table)
 
 
 def solution(mesh):

time: 70.7 us -> 57.3 us (0.81)
  the two profiles are of different devices: /device:TPU:10 before, /device:TPU:6 now
where the time goes in v2:
time: 57.3 us; the launch traced here: 57.1 us
  Pallas kernels  54.1 us (94%)
  local copies, waits for them, and re-layouts  2.9 us (5%)
    pallas_call x1, Pallas kernels, on_device(): pl.pallas_call(functools.partial(kernel, nc, nt), out_shape=jax.ShapeDtyp...  54.1 us
    unnamed x2, local copies, waits for them, and re-layouts  2.9 us

profile of v2, /device:TPU:6, one launch (start us, length us, event | category | flops | bytes accessed | tf_op | source)
XLA Modules:
  0.0 57.1 jit_solution(10138278168698367255)
XLA Ops:
  0.0 1.4 %copy.5.w_ref = f32[2,64,16]{2,1,0:T(8,128)} copy(f32[2,64,16]{1,2,0:T(8,128)} %param.6) | data formatting | bytes 16384 | tf_op args[2]
  1.4 54.1 %radar.1 = f32[4,2,8,256]{3,2,1,0:T(8,128)} custom-call(f32[2,2048]{1,0:T(2,128)} %ref_ref.1, f32[2,16,2048]{2,1,0:T(8,128)} %surv_ref.1, f32[2,64,16]{2,1,0:T(8,128)} %copy.5.w_ref, bf16[2,512,512]{2,1,0:T(8,128)(2,1)} %constant.2.clone.table_ref), custom_call_target="tpu_custom_call" | custom-call | tf_op jit(solution)/shard_map/radar/pallas_call | solution.py:377
  55.6 1.5 %copy.7 = f32[4,2,8,256]{3,2,1,0:T(8,128)} copy(f32[4,2,8,256]{3,2,1,0:T(8,128)} %radar.1) | data formatting | bytes 131072

commit v3 on v2

--- a/solution.py
+++ b/solution.py
@@ -107,8 +107,8 @@
 
 
 def kernel(nc, nt, ref_ref, surv_ref, w_ref, table_ref, out_ref,
-           part, core_buf, chip_send, chip_buf, halo, lagt, lag_hi, lag_mid, tap_lo, gm, gm_buf, xm, xm_buf, emb, lg, lg_buf,
-           halo_ss, halo_rs, core_ss, core_rs, rs_ss, rs_rs, gm_ss, gm_rs, xm_ss, xm_rs, lg_ss, lg_rs):
+           part, core_buf, chip_send, chip_buf, halo, lag_hi, lag_mid, tap_lo, gm, gm_buf, xm, xm_buf, emb, lg, lg_buf,
+           reach, halo_ss, halo_rs, core_ss, core_rs, rs_ss, rs_rs, gm_ss, gm_rs, xm_ss, xm_rs, lg_ss, lg_rs):
     c = lax.axis_index("chan")
     d = lax.axis_index("tm")
     length = ref_ref.shape[1]
@@ -130,12 +130,19 @@
         pl.semaphore_signal(barrier, inc=1, device_id={"chan": chan_peer(j)}, device_id_type=MESH)
         return 0
 
-    def greet_tm(j, _):
-        pl.semaphore_signal(barrier, inc=1, device_id={"tm": tm_peer(j)}, device_id_type=MESH)
-        return 0
-
-    lax.fori_loop(0, nt - 1, greet_tm, 0)
+    def tm_near(offset):
+        return {"tm": lax.rem(d + offset + nt, nt)}
+
     lax.fori_loop(0, nc - 1, greet_chan, 0)
+    for offset in (-2, -1, 1, 2):
+        pl.semaphore_signal(barrier, inc=1, device_id=tm_near(offset), device_id_type=MESH)
+
+    def reach_signal(i):
+        for offset in (-(2 << i), 2 << i):
+            pl.semaphore_signal(reach.at[i], inc=1, device_id=tm_near(offset), device_id_type=MESH)
+
+    def reach_wait(i):
+        pl.semaphore_wait(reach.at[i], 2)
 
     w_re, w_im = w_ref[0], w_ref[1]
     survey = jnp.concatenate([surv_ref[0], surv_ref[1]], 0)
@@ -145,7 +152,8 @@
         rows = slice(beams * owner, beams * (owner + 1))
         part[owner % 2, owner // 2] = jnp.concatenate([part_re[rows], part_im[rows]], 0)
 
-    pl.semaphore_wait(barrier, nt - 1 + nc - 1)
+    pl.semaphore_wait(barrier, nc - 1 + 4)
+    reach_signal(0)
 
     right = lax.rem(d + 1, nt)
     halo_copy = pltpu.make_async_remote_copy(
@@ -183,20 +191,39 @@
     core_copy(chip).wait_recv()
     chip_buf[chip] = part[core, chip] + core_buf[chip]
 
+    reach_wait(0)
+    reach_signal(1)
+
     halo_copy.wait()
     ref = ref_ref[...]
     before = jnp.where(d == 0, 0.0, halo[...])
     extended = jnp.concatenate([before, ref], 1)
+
+    def lags_of(p, first, count):
+        row = jnp.broadcast_to(extended[p : p + 1, :], (count, HALO + length))
+        return pltpu.roll(row, first, 1, stride=1, stride_axis=0)[:, HALO:]
+
+    taps = jnp.concatenate([lags_of(0, 0, TAPS), lags_of(1, 0, TAPS)], 0)
+    taps_hi, taps_mid, taps_lo = split(taps, 3)
     for p in range(2):
-        shifted = pltpu.roll(
-            jnp.broadcast_to(extended[p : p + 1, :], (LAGS, HALO + length)), 0, 1, stride=1, stride_axis=0)
-        lagt[p] = shifted[:, HALO:]
-    taps = jnp.concatenate([lagt[0, :TAPS, :], lagt[1, :TAPS, :]], 0)
+        lag_hi[LAGS * p : LAGS * p + TAPS] = taps_hi[TAPS * p : TAPS * (p + 1)].astype(jnp.bfloat16)
+        lag_mid[LAGS * p : LAGS * p + TAPS] = taps_mid[TAPS * p : TAPS * (p + 1)].astype(jnp.bfloat16)
+    tap_lo[...] = taps_lo.astype(jnp.bfloat16)
+    reach_wait(1)
+    reach_signal(2)
+    tap_terms = [jnp.concatenate([lag_hi[:TAPS], lag_hi[LAGS : LAGS + TAPS]], 0),
+                 jnp.concatenate([lag_mid[:TAPS], lag_mid[LAGS : LAGS + TAPS]], 0), tap_lo[...]]
+
+    def lag_products(rows8):
+        terms = jnp.concatenate(split(rows8, 3), 0).astype(jnp.bfloat16)
+        cols = sum(bdot_nt(term, terms) for term in tap_terms)
+        turned = jnp.concatenate([cols, jnp.zeros((2 * TAPS, 128 - cols.shape[1]), jnp.float32)], 1).T
+        return turned[:8] + turned[8:16] + turned[16:24]
 
     row8 = iota((8, length), 0)
     mark = jnp.where((iota((8, length), 1) == length - 1) & (d == nt - 1), 1.0, 0.0)
     probe = jnp.where(row8 == 0, ref[0:1], jnp.where(row8 == 1, ref[1:2], jnp.where(row8 == 2, mark, 0.0)))
-    g_raw = dot_nt(probe, taps)
+    g_raw = lag_products(probe)
     g_conj = conj_pack(g_raw[0:1], g_raw[1:2])
     gm[0:1, :] = jnp.where(iota(g_conj.shape, 1) < TAPS, g_conj, -g_conj)
     gm[1:2, :] = g_raw[2:3]
@@ -239,16 +266,14 @@
 
         lax.fori_loop(0, nt - 1, body, 0)
 
+    reach_wait(2)
     tm_start(gm_copy)
     gm_buf[d] = gm[...]
 
     for p in range(2):
-        hi, mid, lo = split(lagt[p], 3)
-        lag_hi[LAGS * p : LAGS * (p + 1)] = hi.astype(jnp.bfloat16)
-        lag_mid[LAGS * p : LAGS * (p + 1)] = mid.astype(jnp.bfloat16)
-        tap_lo[TAPS * p : TAPS * (p + 1)] = lo[:TAPS].astype(jnp.bfloat16)
-    tap_terms = [jnp.concatenate([lag_hi[:TAPS], lag_hi[LAGS : LAGS + TAPS]], 0),
-                 jnp.concatenate([lag_mid[:TAPS], lag_mid[LAGS : LAGS + TAPS]], 0), tap_lo[...]]
+        hi, mid = split(lags_of(p, TAPS, LAGS - TAPS), 2)
+        lag_hi[LAGS * p + TAPS : LAGS * (p + 1)] = hi.astype(jnp.bfloat16)
+        lag_mid[LAGS * p + TAPS : LAGS * (p + 1)] = mid.astype(jnp.bfloat16)
 
     def rs_wait(j, _):
         peer = chip_peer(j)
@@ -260,10 +285,7 @@
     for source in range(1, chips):
         total = total + chip_buf[source]
 
-    total_terms = jnp.concatenate(split(total, 3), 0).astype(jnp.bfloat16)
-    x_cols = sum(bdot_nt(term, total_terms) for term in tap_terms)
-    x_rows = jnp.concatenate([x_cols, jnp.zeros((2 * TAPS, 128 - x_cols.shape[1]), jnp.float32)], 1).T
-    x_raw = x_rows[: 2 * beams] + x_rows[2 * beams : 4 * beams] + x_rows[4 * beams : 6 * beams]
+    x_raw = lag_products(total)
     xm[...] = conj_pack(x_raw[:beams], x_raw[beams:])
     tm_start(xm_copy)
     xm_buf[d] = xm[...]
@@ -298,29 +320,62 @@
             base = cols * order + 2 * blocks * m
             pair = jnp.concatenate([spread(term[m : m + 1]), spread(term[beams + m : beams + m + 1])], 0)
             emb[base : base + 2 * blocks, :] = pair.astype(jnp.bfloat16)
-    products = bdot_nt(lag_hi[...], emb[...]) + bdot_nt(lag_mid[...], emb[...])
-    products = products + pltpu.roll(products, cols, 1)
-    with_re, with_im = products[:LAGS], products[LAGS:]
-    real_lane = iota((LAGS, 2 * cols), 1) % (2 * blocks) < blocks
-    lagged = with_re + jnp.where(
-        real_lane, pltpu.roll(with_im, 2 * cols - blocks, 1), -pltpu.roll(with_im, blocks, 1))
     own = LAGS // nt
-    for dest in range(nt):
-        lg[dest] = lagged[own * dest : own * (dest + 1), :]
-    tm_start(lg_copy)
+    half = own // 2
+    groups = 4
+    span = LAGS // groups
+    targets = nt // groups
+    real_lane = iota((span, 2 * cols), 1) % (2 * blocks) < blocks
+    low_lane = iota((half, 2 * cols), 1) < cols
+
+    def correlate(step, _):
+        group = lax.rem(d // targets + groups // 2 + step, groups)
+
+        def both_terms_of(p):
+            rows = pl.ds(pl.multiple_of(LAGS * p + span * group, span), span)
+            sums = bdot_nt(lag_hi[rows, :], emb[...]) + bdot_nt(lag_mid[rows, :], emb[...])
+            return sums + pltpu.roll(sums, cols, 1)
+
+        with_re, with_im = both_terms_of(0), both_terms_of(1)
+        lagged = with_re + jnp.where(
+            real_lane, pltpu.roll(with_im, 2 * cols - blocks, 1), -pltpu.roll(with_im, blocks, 1))
+        for i in range(targets):
+            lg[targets * group + i] = jnp.where(
+                low_lane, lagged[own * i : own * i + half], lagged[own * i + half : own * (i + 1)])
+
+        def send(i, _):
+            peer = targets * group + i
+
+            @pl.when(peer != d)
+            def _():
+                lg_copy(peer, d).start()
+
+            return 0
+
+        lax.fori_loop(0, targets, send, 0)
+        return 0
+
+    lax.fori_loop(0, groups, correlate, 0)
     lg_buf[d] = lg[d]
     tm_wait_recv(lg_copy)
 
     wide = 2 * blocks
     group = 128 // wide
     slot_of = iota((own, 128), 1) // wide
+    upper_row = iota((own, 128), 0) < half
+
+    def received(s):
+        twice = jnp.concatenate([lg_buf[s], lg_buf[s]], 0)
+        return jnp.where(upper_row, twice, pltpu.roll(twice, 64, 1))
+
+    arrived = [received(s) for s in range(nt)]
     rows = []
     for m in range(beams):
         pieces = []
         for start in range(0, nt, group):
             acc = jnp.zeros((own, 128), jnp.float32)
             for s in range(group):
-                moved = pltpu.roll(lg_buf[start + s], (wide * (s - m)) % 128, 1)
+                moved = pltpu.roll(arrived[start + s], (wide * (s - m)) % 128, 1)
                 acc = jnp.where(slot_of == s, moved, acc)
             pieces.append(acc)
         rows.append(jnp.concatenate(pieces, 1))
@@ -385,7 +440,6 @@
             pltpu.VMEM((chips, 2 * beams, length), f32),
             pltpu.VMEM((chips, 2 * beams, length), f32),
             pltpu.VMEM((2, HALO), f32),
-            pltpu.VMEM((2, LAGS, length), f32),
             pltpu.VMEM((2 * LAGS, length), bf16),
             pltpu.VMEM((2 * LAGS, length), bf16),
             pltpu.VMEM((2 * TAPS, length), bf16),
@@ -394,8 +448,9 @@
             pltpu.VMEM((beams, 2 * TAPS), f32),
             pltpu.VMEM((nt, beams, 2 * TAPS), f32),
             pltpu.VMEM((4 * blocks * beams, length), bf16),
-            pltpu.VMEM((nt, own, 128), f32),
-            pltpu.VMEM((nt, own, 128), f32),
+            pltpu.VMEM((nt, own // 2, 128), f32),
+            pltpu.VMEM((nt, own // 2, 128), f32),
+            pltpu.SemaphoreType.REGULAR((3,)),
             pltpu.SemaphoreType.DMA,
             pltpu.SemaphoreType.DMA,
             pltpu.SemaphoreType.DMA((chips,)),

time: 57.3 us -> 54.3 us (0.948)
  the two profiles are of different devices: /device:TPU:6 before, /device:TPU:32 now
where the time goes in v3:
time: 54.3 us; the launch traced here: 54 us
  Pallas kernels  51.1 us (94%)
  local copies, waits for them, and re-layouts  2.9 us (5%)
    pallas_call x1, Pallas kernels, on_device(): pl.pallas_call(functools.partial(kernel, nc, nt), out_shape=jax.ShapeDtyp...  51.1 us
    unnamed x2, local copies, waits for them, and re-layouts  2.9 us

profile of v3, /device:TPU:32, one launch (start us, length us, event | category | flops | bytes accessed | tf_op | source)
XLA Modules:
  0.0 54.0 jit_solution(2030516117984787270)
XLA Ops:
  0.0 1.4 %copy.5.w_ref = f32[2,64,16]{2,1,0:T(8,128)} copy(f32[2,64,16]{1,2,0:T(8,128)} %param.6) | data formatting | bytes 16384 | tf_op args[2]
  1.4 51.1 %radar.1 = f32[4,2,8,256]{3,2,1,0:T(8,128)} custom-call(f32[2,2048]{1,0:T(2,128)} %ref_ref.1, f32[2,16,2048]{2,1,0:T(8,128)} %surv_ref.1, f32[2,64,16]{2,1,0:T(8,128)} %copy.5.w_ref, bf16[2,512,512]{2,1,0:T(8,128)(2,1)} %constant.2.clone.table_ref), custom_call_target="tpu_custom_call" | custom-call | tf_op jit(solution)/shard_map/radar/pallas_call | solution.py:432
  52.6 1.5 %copy.7 = f32[4,2,8,256]{3,2,1,0:T(8,128)} copy(f32[4,2,8,256]{3,2,1,0:T(8,128)} %radar.1) | data formatting | bytes 131072

commit v4 on v3

--- a/solution.py
+++ b/solution.py
@@ -76,12 +76,13 @@
         r1 = jnp.where(here, jnp.where(at1, 1.0, 0.0), m[k + 1 : k + 2])
         t0 = pltpu.roll(r0, n, 1) * flip
         t1 = pltpu.roll(r1, n, 1) * flip
-        a, d, br, bi = a * inv, d * inv, br * inv, bi * inv
         n0 = d * r0 - br * r1 - bi * t1
         u0 = d * t0 - br * t1 + bi * r1
         n1 = a * r1 - br * r0 + bi * t0
         u1 = a * t1 - br * t0 - bi * r0
-        rest = (jnp.where(here, 0.0, m) - c0r * n0 - c1r * n1) - (c0i * u0 + c1i * u1)
+        change = (c0r * n0 + c1r * n1) + (c0i * u0 + c1i * u1)
+        rest = jnp.where(here, 0.0, m) - inv * change
+        n0, n1 = inv * n0, inv * n1
         m = jnp.where(row_id == k, n0, jnp.where(row_id == k + 1, n1, rest))
     return m
 
@@ -106,9 +107,9 @@
     return toeplitz - (square[:n] + sign * pltpu.roll(square[n:], n, 1))
 
 
-def kernel(nc, nt, ref_ref, surv_ref, w_ref, table_ref, out_ref,
-           part, core_buf, chip_send, chip_buf, halo, lag_hi, lag_mid, tap_lo, gm, gm_buf, xm, xm_buf, emb, lg, lg_buf,
-           reach, halo_ss, halo_rs, core_ss, core_rs, rs_ss, rs_rs, gm_ss, gm_rs, xm_ss, xm_rs, lg_ss, lg_rs):
+def kernel(nc, nt, ref_hbm, surv_hbm, w_hbm, table_hbm, out_ref,
+           ref_ref, surv_ref, w_ref, table, part, core_buf, chip_send, chip_buf, halo, lag_hi, lag_mid, tap_lo, gm, gm_buf, xm, xm_buf, emb, lg, lg_buf,
+           reach, halo_ss, halo_rs, core_ss, core_rs, rs_ss, rs_rs, gm_ss, gm_rs, xm_ss, xm_rs, lg_ss, lg_rs, in_sems):
     c = lax.axis_index("chan")
     d = lax.axis_index("tm")
     length = ref_ref.shape[1]
@@ -144,10 +145,30 @@
     def reach_wait(i):
         pl.semaphore_wait(reach.at[i], 2)
 
+    loads = [
+        pltpu.make_async_copy(source, target, in_sems.at[i])
+        for i, (source, target) in enumerate(
+            ((w_hbm, w_ref), (surv_hbm, surv_ref), (ref_hbm, ref_ref), (table_hbm, table)))
+    ]
+    for load in loads:
+        load.start()
+    table_copy = loads.pop()
+    for load in loads:
+        load.wait()
+
     w_re, w_im = w_ref[0], w_ref[1]
+    weights_t = jnp.concatenate(
+        [jnp.concatenate([w_re, w_im], 1), jnp.concatenate([-w_im, w_re], 1)], 0)
+    w_hi, w_mid, w_lo = split(weights_t, 3)
     survey = jnp.concatenate([surv_ref[0], surv_ref[1]], 0)
-    part_re = dot(jnp.concatenate([w_re, -w_im], 1), survey)
-    part_im = dot(jnp.concatenate([w_im, w_re], 1), survey)
+    s_hi, s_mid, s_lo = split(survey, 3)
+    left = jnp.concatenate([w_hi, w_hi, w_mid, w_hi, w_mid, w_lo], 0)
+    depth = left.shape[0]
+    left = jnp.concatenate([left, jnp.zeros((256 - depth, left.shape[1]), jnp.float32)], 0).T
+    right_side = jnp.concatenate(
+        [s_hi, s_mid, s_hi, s_lo, s_mid, s_hi, jnp.zeros((256 - depth, length), jnp.float32)], 0)
+    partial = bdot(left.astype(jnp.bfloat16), right_side.astype(jnp.bfloat16))
+    part_re, part_im = partial[: beams * nc], partial[beams * nc :]
     for owner in range(nc):
         rows = slice(beams * owner, beams * (owner + 1))
         part[owner % 2, owner // 2] = jnp.concatenate([part_re[rows], part_im[rows]], 0)
@@ -186,10 +207,6 @@
         chip_send[peer] = part[core, peer] + core_buf[peer]
         rs_copy(peer, chip).start()
         return 0
-
-    lax.fori_loop(0, chips - 1, rs_start, 0)
-    core_copy(chip).wait_recv()
-    chip_buf[chip] = part[core, chip] + core_buf[chip]
 
     reach_wait(0)
     reach_signal(1)
@@ -209,8 +226,13 @@
         lag_hi[LAGS * p : LAGS * p + TAPS] = taps_hi[TAPS * p : TAPS * (p + 1)].astype(jnp.bfloat16)
         lag_mid[LAGS * p : LAGS * p + TAPS] = taps_mid[TAPS * p : TAPS * (p + 1)].astype(jnp.bfloat16)
     tap_lo[...] = taps_lo.astype(jnp.bfloat16)
+
+    lax.fori_loop(0, chips - 1, rs_start, 0)
     reach_wait(1)
     reach_signal(2)
+    core_copy(chip).wait_recv()
+    chip_buf[chip] = part[core, chip] + core_buf[chip]
+
     tap_terms = [jnp.concatenate([lag_hi[:TAPS], lag_hi[LAGS : LAGS + TAPS]], 0),
                  jnp.concatenate([lag_mid[:TAPS], lag_mid[LAGS : LAGS + TAPS]], 0), tap_lo[...]]
 
@@ -230,41 +252,31 @@
 
     def gm_copy(peer, slot):
         return pltpu.make_async_remote_copy(
-            src_ref=gm, dst_ref=gm_buf.at[slot], send_sem=gm_ss.at[peer], recv_sem=gm_rs.at[slot],
+            src_ref=gm, dst_ref=gm_buf.at[slot], send_sem=gm_ss, recv_sem=gm_rs,
             device_id={"tm": peer}, device_id_type=MESH)
 
     def xm_copy(peer, slot):
         return pltpu.make_async_remote_copy(
-            src_ref=xm, dst_ref=xm_buf.at[slot], send_sem=xm_ss.at[peer], recv_sem=xm_rs.at[slot],
+            src_ref=xm, dst_ref=xm_buf.at[slot], send_sem=xm_ss, recv_sem=xm_rs,
             device_id={"tm": peer}, device_id_type=MESH)
 
     def lg_copy(peer, slot):
         return pltpu.make_async_remote_copy(
-            src_ref=lg.at[peer], dst_ref=lg_buf.at[slot], send_sem=lg_ss.at[peer], recv_sem=lg_rs.at[slot],
+            src_ref=lg.at[peer], dst_ref=lg_buf.at[slot], send_sem=lg_ss, recv_sem=lg_rs,
             device_id={"tm": peer}, device_id_type=MESH)
 
     def tm_start(copy):
-        def body(j, _):
+        for j in range(nt - 1):
             copy(tm_peer(j), d).start()
-            return 0
-
-        lax.fori_loop(0, nt - 1, body, 0)
-
-    def tm_wait_recv(copy):
-        def body(j, _):
-            peer = tm_peer(j)
-            copy(peer, peer).wait_recv()
-            return 0
-
-        lax.fori_loop(0, nt - 1, body, 0)
-
-    def tm_wait_send(copy):
-        def body(j, _):
-            peer = tm_peer(j)
-            copy(peer, peer).wait_send()
-            return 0
-
-        lax.fori_loop(0, nt - 1, body, 0)
+
+    def all_of(buf, send_sem, recv_sem):
+        return pltpu.make_async_remote_copy(
+            src_ref=buf.at[pl.ds(0, nt - 1)], dst_ref=buf.at[pl.ds(0, nt - 1)], send_sem=send_sem, recv_sem=recv_sem,
+            device_id={"tm": tm_peer(0)}, device_id_type=MESH)
+
+    gm_all = all_of(gm_buf, gm_ss, gm_rs)
+    xm_all = all_of(xm_buf, xm_ss, xm_rs)
+    lg_all = all_of(lg_buf, lg_ss, lg_rs)
 
     reach_wait(2)
     tm_start(gm_copy)
@@ -290,7 +302,7 @@
     tm_start(xm_copy)
     xm_buf[d] = xm[...]
 
-    tm_wait_recv(gm_copy)
+    gm_all.wait_recv()
     g_sum = jnp.sum(gm_buf[...], axis=0)
     gram = gram_matrix(g_sum[0:1], g_sum[1:2])
     level = 1.0 / gram[0:1, 0:1]
@@ -298,7 +310,7 @@
     inverse = widen(hermitian_inverse(gram))
     gram_wide = widen(gram)
 
-    tm_wait_recv(xm_copy)
+    xm_all.wait_recv()
     x = jnp.sum(xm_buf[...], axis=0) * level
     weights = dot(x, inverse)
     weights = weights + dot(x - dot(weights, gram_wide), inverse)
@@ -357,7 +369,7 @@
 
     lax.fori_loop(0, groups, correlate, 0)
     lg_buf[d] = lg[d]
-    tm_wait_recv(lg_copy)
+    lg_all.wait_recv()
 
     wide = 2 * blocks
     group = 128 // wide
@@ -382,15 +394,16 @@
     stacked = jnp.concatenate(rows, 0)
     height = own * beams
     stacked_terms = jnp.concatenate(split(stacked, 2), 0).astype(jnp.bfloat16)
-    spectrum = bdot(stacked_terms, table_ref[0]) + bdot(stacked_terms, table_ref[1])
+    table_copy.wait()
+    spectrum = bdot(stacked_terms, table[0]) + bdot(stacked_terms, table[1])
     spectrum = spectrum[:height] + spectrum[height:]
     for m in range(beams):
         for part_id in range(2):
             out_ref[m, part_id] = spectrum[own * m : own * (m + 1), DOPPLER * part_id : DOPPLER * (part_id + 1)]
 
-    tm_wait_send(gm_copy)
-    tm_wait_send(xm_copy)
-    tm_wait_send(lg_copy)
+    gm_all.wait_send()
+    xm_all.wait_send()
+    lg_all.wait_send()
 
     def rs_drain(j, _):
         peer = chip_peer(j)
@@ -432,9 +445,13 @@
     return pl.pallas_call(
         functools.partial(kernel, nc, nt),
         out_shape=jax.ShapeDtypeStruct((beams, 2, own, DOPPLER), f32),
-        in_specs=[vmem] * 4,
+        in_specs=[pl.BlockSpec(memory_space=pltpu.HBM)] * 4,
         out_specs=vmem,
         scratch_shapes=[
+            pltpu.VMEM((2, length), f32),
+            pltpu.VMEM((2, chans, length), f32),
+            pltpu.VMEM((2, chans, beams * nc), f32),
+            pltpu.VMEM((2, 2 * nt * blocks, 2 * DOPPLER), bf16),
             pltpu.VMEM((2, chips, 2 * beams, length), f32),
             pltpu.VMEM((chips, 2 * beams, length), f32),
             pltpu.VMEM((chips, 2 * beams, length), f32),
@@ -457,16 +474,17 @@
             pltpu.SemaphoreType.DMA((chips,)),
             pltpu.SemaphoreType.DMA((chips,)),
             pltpu.SemaphoreType.DMA((chips,)),
-            pltpu.SemaphoreType.DMA((nt,)),
-            pltpu.SemaphoreType.DMA((nt,)),
-            pltpu.SemaphoreType.DMA((nt,)),
-            pltpu.SemaphoreType.DMA((nt,)),
-            pltpu.SemaphoreType.DMA((nt,)),
-            pltpu.SemaphoreType.DMA((nt,)),
+            pltpu.SemaphoreType.DMA,
+            pltpu.SemaphoreType.DMA,
+            pltpu.SemaphoreType.DMA,
+            pltpu.SemaphoreType.DMA,
+            pltpu.SemaphoreType.DMA,
+            pltpu.SemaphoreType.DMA,
+            pltpu.SemaphoreType.DMA((4,)),
         ],
         compiler_params=pltpu.CompilerParams(collective_id=0, has_side_effects=True, vmem_limit_bytes=60 << 20),
         name="radar",
-    )(ref_signal, surveillance, steering, table)
+    )(ref_signal, surveillance, jnp.swapaxes(steering, 1, 2), table)
 
 
 def solution(mesh):

time: 54.3 us -> 47.1 us (0.87)
  the two profiles are of different devices: /device:TPU:32 before, /device:TPU:6 now
where the time goes in v4:
time: 47.1 us; the launch traced here: 46.9 us
  Pallas kernels  45.4 us (96%)
  local copies, waits for them, and re-layouts  1.47 us (3%)
    pallas_call x1, Pallas kernels, on_device(): pl.pallas_call(functools.partial(kernel, nc, nt), out_shape=jax.ShapeDtyp...  45.4 us
    unnamed x1, local copies, waits for them, and re-layouts  1.47 us

profile of v4, /device:TPU:6, one launch (start us, length us, event | category | flops | bytes accessed | tf_op | source)
XLA Modules:
  0.0 46.9 jit_solution(3030180027973820559)
XLA Ops:
  0.0 45.4 %radar.1 = f32[4,2,8,256]{3,2,1,0:T(8,128)} custom-call(f32[2,2048]{1,0:T(2,128)} %ref_hbm.1, f32[2,16,2048]{2,1,0:T(8,128)} %surv_hbm.1, f32[2,16,64]{2,1,0:T(8,128)} %bitcast.1, bf16[2,512,512]{2,1,0:T(8,128)(2,1)} %constant.2.clone.table_hbm), custom_call_target="tpu_custom_call" | custom-call | tf_op jit(solution)/shard_map/radar/pallas_call | solution.py:445
  45.4 1.5 %copy.6 = f32[4,2,8,256]{3,2,1,0:T(8,128)} copy(f32[4,2,8,256]{3,2,1,0:T(8,128)} %radar.1) | data formatting | bytes 131072

commit v5 on v4

--- a/solution.py
+++ b/solution.py
@@ -59,32 +59,51 @@
     return jnp.concatenate([packed * sign, pltpu.roll(packed, half, 1)], 0)
 
 
-def hermitian_inverse(m):
+def conj_product(left, right):
+    n = left.shape[1] // 2
+    pad = jnp.zeros((2 * n - left.shape[0], 2 * n), jnp.float32)
+    square = dot(jnp.concatenate([left, pad], 0).T, jnp.concatenate([right, pad], 0))
+    sign = jnp.where(iota((n, 2 * n), 1) < n, 1.0, -1.0)
+    return square[:n] + sign * pltpu.roll(square[n:], n, 1)
+
+
+def hermitian_inverse(m, scaled):
     n = m.shape[0]
-    wide = (n, 2 * n)
+    tile = 8
+    blocks = [m[tile * i : tile * (i + 1)] for i in range(n // tile)]
     lane = iota((1, 2 * n), 1)
-    row_id = iota((n, 1), 0)
+    row_id = iota((tile, 1), 0)
     flip = jnp.where(lane < n, -1.0, 1.0)
     for k in range(0, n, 2):
-        c0r, c1r, c0i, c1i = (jnp.broadcast_to(m[:, j : j + 1], wide) for j in (k, k + 1, n + k, n + k + 1))
-        a, d = c0r[k : k + 1], c1r[k + 1 : k + 2]
-        br, bi = c1r[k : k + 1], c1i[k : k + 1]
+        home, at = blocks[k // tile], k % tile
+        p0, p1 = home[at : at + 1], home[at + 1 : at + 2]
+        a, br, bi = (jnp.broadcast_to(p0[:, j : j + 1], (1, 2 * n)) for j in (k, k + 1, n + k + 1))
+        d = jnp.broadcast_to(p1[:, k + 1 : k + 2], (1, 2 * n))
         inv = 1.0 / (a * d - (br * br + bi * bi))
         at0, at1 = lane == k, lane == k + 1
         here = at0 | at1 | (lane == n + k) | (lane == n + k + 1)
-        r0 = jnp.where(here, jnp.where(at0, 1.0, 0.0), m[k : k + 1])
-        r1 = jnp.where(here, jnp.where(at1, 1.0, 0.0), m[k + 1 : k + 2])
+        r0 = jnp.where(here, jnp.where(at0, 1.0, 0.0), p0)
+        r1 = jnp.where(here, jnp.where(at1, 1.0, 0.0), p1)
         t0 = pltpu.roll(r0, n, 1) * flip
         t1 = pltpu.roll(r1, n, 1) * flip
         n0 = d * r0 - br * r1 - bi * t1
         u0 = d * t0 - br * t1 + bi * r1
         n1 = a * r1 - br * r0 + bi * t0
         u1 = a * t1 - br * t0 - bi * r0
-        change = (c0r * n0 + c1r * n1) + (c0i * u0 + c1i * u1)
-        rest = jnp.where(here, 0.0, m) - inv * change
-        n0, n1 = inv * n0, inv * n1
-        m = jnp.where(row_id == k, n0, jnp.where(row_id == k + 1, n1, rest))
-    return m
+        scaled[k : k + 1] = inv * n0
+        scaled[k + 1 : k + 2] = inv * n1
+        for i in range((k + 2) // tile, n // tile):
+            block = blocks[i]
+            c0r, c1r, c0i, c1i = (
+                jnp.broadcast_to(block[:, j : j + 1], (tile, 2 * n)) for j in (k, k + 1, n + k, n + k + 1))
+            change = (c0r * n0 + c1r * n1) + (c0i * u0 + c1i * u1)
+            rest = jnp.where(here, 0.0, block) - inv * change
+            blocks[i] = rest if tile * i > k + 1 else jnp.where(row_id > at + 1, rest, block)
+    row = iota((n, 2 * n), 0)
+    col = iota((n, 2 * n), 1) % n
+    whole = jnp.concatenate(blocks, 0)
+    lower = jnp.where(col < row - row % 2, whole, jnp.where(iota((n, 2 * n), 1) == row, 1.0, 0.0))
+    return conj_product(lower, jnp.where(col < row - row % 2 + 2, scaled[...], 0.0))
 
 
 def gram_matrix(g_row, e_row):
@@ -92,7 +111,6 @@
     row = iota((n, 2 * n), 0)
     lane = iota((n, 2 * n), 1)
     col = lane % n
-    sign = jnp.where(lane < n, 1.0, -1.0)
 
     def shifted(v):
         return pltpu.roll(jnp.broadcast_to(v, (n, 2 * n)), 0, 1, stride=1, stride_axis=0)
@@ -102,13 +120,11 @@
     lower = flipped[:n] - pltpu.roll(flipped[n:], n, 1)
     toeplitz = jnp.where(col >= row, upper, lower)
     tail = jnp.where((col >= row) & (row >= 1), shifted(e_row), 0.0)
-    tail = jnp.concatenate([tail, jnp.zeros_like(tail)], 0)
-    square = dot(tail.T, tail)
-    return toeplitz - (square[:n] + sign * pltpu.roll(square[n:], n, 1))
+    return toeplitz - conj_product(tail, tail)
 
 
 def kernel(nc, nt, ref_hbm, surv_hbm, w_hbm, table_hbm, out_ref,
-           ref_ref, surv_ref, w_ref, table, part, core_buf, chip_send, chip_buf, halo, lag_hi, lag_mid, tap_lo, gm, gm_buf, xm, xm_buf, emb, lg, lg_buf,
+           ref_ref, surv_ref, w_ref, table, part, core_buf, chip_send, chip_buf, halo, lag_tab, gm, gm_buf, xm, xm_buf, scaled, emb, lg, lg_buf,
            reach, halo_ss, halo_rs, core_ss, core_rs, rs_ss, rs_rs, gm_ss, gm_rs, xm_ss, xm_rs, lg_ss, lg_rs, in_sems):
     c = lax.axis_index("chan")
     d = lax.axis_index("tm")
@@ -134,7 +150,8 @@
     def tm_near(offset):
         return {"tm": lax.rem(d + offset + nt, nt)}
 
-    lax.fori_loop(0, nc - 1, greet_chan, 0)
+    for j in range(nc - 1):
+        greet_chan(j, 0)
     for offset in (-2, -1, 1, 2):
         pl.semaphore_signal(barrier, inc=1, device_id=tm_near(offset), device_id_type=MESH)
 
@@ -199,7 +216,8 @@
         core_copy(chip_peer(j)).start()
         return 0
 
-    lax.fori_loop(0, chips, core_start, 0)
+    for j in range(chips):
+        core_start(j, 0)
 
     def rs_start(j, _):
         peer = chip_peer(j)
@@ -222,23 +240,22 @@
 
     taps = jnp.concatenate([lags_of(0, 0, TAPS), lags_of(1, 0, TAPS)], 0)
     taps_hi, taps_mid, taps_lo = split(taps, 3)
-    for p in range(2):
-        lag_hi[LAGS * p : LAGS * p + TAPS] = taps_hi[TAPS * p : TAPS * (p + 1)].astype(jnp.bfloat16)
-        lag_mid[LAGS * p : LAGS * p + TAPS] = taps_mid[TAPS * p : TAPS * (p + 1)].astype(jnp.bfloat16)
-    tap_lo[...] = taps_lo.astype(jnp.bfloat16)
-
-    lax.fori_loop(0, chips - 1, rs_start, 0)
+    for order, term in enumerate((taps_lo, taps_hi, taps_mid)):
+        lag_tab[2 * TAPS * order : 2 * TAPS * (order + 1)] = term.astype(jnp.bfloat16)
+
+    for j in range(chips - 1):
+        rs_start(j, 0)
     reach_wait(1)
     reach_signal(2)
     core_copy(chip).wait_recv()
     chip_buf[chip] = part[core, chip] + core_buf[chip]
 
-    tap_terms = [jnp.concatenate([lag_hi[:TAPS], lag_hi[LAGS : LAGS + TAPS]], 0),
-                 jnp.concatenate([lag_mid[:TAPS], lag_mid[LAGS : LAGS + TAPS]], 0), tap_lo[...]]
+    tap_rows = 6 * TAPS
 
     def lag_products(rows8):
         terms = jnp.concatenate(split(rows8, 3), 0).astype(jnp.bfloat16)
-        cols = sum(bdot_nt(term, terms) for term in tap_terms)
+        cols = bdot_nt(lag_tab[:tap_rows], terms)
+        cols = cols[: 2 * TAPS] + cols[2 * TAPS : 4 * TAPS] + cols[4 * TAPS :]
         turned = jnp.concatenate([cols, jnp.zeros((2 * TAPS, 128 - cols.shape[1]), jnp.float32)], 1).T
         return turned[:8] + turned[8:16] + turned[16:24]
 
@@ -284,15 +301,19 @@
 
     for p in range(2):
         hi, mid = split(lags_of(p, TAPS, LAGS - TAPS), 2)
-        lag_hi[LAGS * p + TAPS : LAGS * (p + 1)] = hi.astype(jnp.bfloat16)
-        lag_mid[LAGS * p + TAPS : LAGS * (p + 1)] = mid.astype(jnp.bfloat16)
+        for group in range(1, LAGS // TAPS):
+            rows = slice(TAPS * (group - 1), TAPS * group)
+            base = 2 * TAPS + 4 * TAPS * group + TAPS * p
+            lag_tab[base : base + TAPS] = hi[rows].astype(jnp.bfloat16)
+            lag_tab[base + 2 * TAPS : base + 3 * TAPS] = mid[rows].astype(jnp.bfloat16)
 
     def rs_wait(j, _):
         peer = chip_peer(j)
         rs_copy(peer, peer).wait_recv()
         return 0
 
-    lax.fori_loop(0, chips - 1, rs_wait, 0)
+    for j in range(chips - 1):
+        rs_wait(j, 0)
     total = chip_buf[0]
     for source in range(1, chips):
         total = total + chip_buf[source]
@@ -307,7 +328,7 @@
     gram = gram_matrix(g_sum[0:1], g_sum[1:2])
     level = 1.0 / gram[0:1, 0:1]
     gram = gram * level
-    inverse = widen(hermitian_inverse(gram))
+    inverse = widen(hermitian_inverse(gram, scaled))
     gram_wide = widen(gram)
 
     xm_all.wait_recv()
@@ -318,7 +339,7 @@
     sign = jnp.where(iota(weights.shape, 1) < TAPS, 1.0, -1.0)
     both = jnp.concatenate([weights * sign, pltpu.roll(weights, TAPS, 1)], 0)
     both_terms = jnp.concatenate(split(both, 3), 0).astype(jnp.bfloat16)
-    model = sum(bdot(both_terms, term) for term in tap_terms)
+    model = bdot(jnp.concatenate([both_terms] * 3, 1), lag_tab[:tap_rows])
     clean = total - (model[: 2 * beams] + model[2 * beams : 4 * beams] + model[4 * beams : 6 * beams])
 
     inside = iota((blocks, length), 1) // BLOCK == iota((blocks, length), 0)
@@ -343,32 +364,41 @@
     def correlate(step, _):
         group = lax.rem(d // targets + groups // 2 + step, groups)
 
-        def both_terms_of(p):
-            rows = pl.ds(pl.multiple_of(LAGS * p + span * group, span), span)
-            sums = bdot_nt(lag_hi[rows, :], emb[...]) + bdot_nt(lag_mid[rows, :], emb[...])
-            return sums + pltpu.roll(sums, cols, 1)
-
-        with_re, with_im = both_terms_of(0), both_terms_of(1)
+        sums = bdot_nt(lag_tab[pl.ds(pl.multiple_of(2 * TAPS + 4 * span * group, 2 * TAPS), 4 * span), :], emb[...])
+        sums = sums[: 2 * span] + sums[2 * span :]
+        sums = sums + pltpu.roll(sums, cols, 1)
+        with_re, with_im = sums[:span], sums[span:]
         lagged = with_re + jnp.where(
             real_lane, pltpu.roll(with_im, 2 * cols - blocks, 1), -pltpu.roll(with_im, blocks, 1))
         for i in range(targets):
             lg[targets * group + i] = jnp.where(
                 low_lane, lagged[own * i : own * i + half], lagged[own * i + half : own * (i + 1)])
 
-        def send(i, _):
+        for i in range(targets):
             peer = targets * group + i
 
             @pl.when(peer != d)
-            def _():
+            def _(peer=peer):
                 lg_copy(peer, d).start()
 
-            return 0
-
-        lax.fori_loop(0, targets, send, 0)
         return 0
 
     lax.fori_loop(0, groups, correlate, 0)
     lg_buf[d] = lg[d]
+    gm_all.wait_send()
+    xm_all.wait_send()
+
+    def rs_drain(j, _):
+        peer = chip_peer(j)
+        rs_copy(peer, peer).wait_send()
+        return 0
+
+    def core_drain(j, _):
+        core_copy(j).wait_send()
+        return 0
+
+    lax.fori_loop(0, chips - 1, rs_drain, 0)
+    lax.fori_loop(0, chips, core_drain, 0)
     lg_all.wait_recv()
 
     wide = 2 * blocks
@@ -401,21 +431,7 @@
         for part_id in range(2):
             out_ref[m, part_id] = spectrum[own * m : own * (m + 1), DOPPLER * part_id : DOPPLER * (part_id + 1)]
 
-    gm_all.wait_send()
-    xm_all.wait_send()
     lg_all.wait_send()
-
-    def rs_drain(j, _):
-        peer = chip_peer(j)
-        rs_copy(peer, peer).wait_send()
-        return 0
-
-    def core_drain(j, _):
-        core_copy(j).wait_send()
-        return 0
-
-    lax.fori_loop(0, chips - 1, rs_drain, 0)
-    lax.fori_loop(0, chips, core_drain, 0)
 
 
 def doppler_table(blocks_total, blocks):
@@ -457,13 +473,12 @@
             pltpu.VMEM((chips, 2 * beams, length), f32),
             pltpu.VMEM((chips, 2 * beams, length), f32),
             pltpu.VMEM((2, HALO), f32),
-            pltpu.VMEM((2 * LAGS, length), bf16),
-            pltpu.VMEM((2 * LAGS, length), bf16),
-            pltpu.VMEM((2 * TAPS, length), bf16),
+            pltpu.VMEM((2 * TAPS + 4 * LAGS, length), bf16),
             pltpu.VMEM((2, 2 * TAPS), f32),
             pltpu.VMEM((nt, 2, 2 * TAPS), f32),
             pltpu.VMEM((beams, 2 * TAPS), f32),
             pltpu.VMEM((nt, beams, 2 * TAPS), f32),
+            pltpu.VMEM((TAPS, 2 * TAPS), f32),
             pltpu.VMEM((4 * blocks * beams, length), bf16),
             pltpu.VMEM((nt, own // 2, 128), f32),
             pltpu.VMEM((nt, own // 2, 128), f32),

time: 47.1 us -> 46.4 us (0.985)
  Pallas kernels: 45.4 us -> 44.8 us
    pallas_call x1, Pallas kernels: 45.4 us -> 44.8 us  [on_device(): pl.pallas_call(functools.partial(kernel, nc, nt), out_shape=jax.ShapeDtyp...]
where the time goes in v5:
time: 46.4 us; the launch traced here: 46.3 us
  Pallas kernels  44.8 us (97%)
  local copies, waits for them, and re-layouts  1.47 us (3%)
    pallas_call x1, Pallas kernels, on_device(): pl.pallas_call(functools.partial(kernel, nc, nt), out_shape=jax.ShapeDtyp...  44.8 us
    unnamed x1, local copies, waits for them, and re-layouts  1.47 us

profile of v5, /device:TPU:6, one launch (start us, length us, event | category | flops | bytes accessed | tf_op | source)
XLA Modules:
  0.0 46.3 jit_solution(11384614409569089827)
XLA Ops:
  0.0 44.8 %radar.1 = f32[4,2,8,256]{3,2,1,0:T(8,128)} custom-call(f32[2,2048]{1,0:T(2,128)} %ref_hbm.1, f32[2,16,2048]{2,1,0:T(8,128)} %surv_hbm.1, f32[2,16,64]{2,1,0:T(8,128)} %bitcast.1, bf16[2,512,512]{2,1,0:T(8,128)(2,1)} %constant.2.clone.table_hbm), custom_call_target="tpu_custom_call" | custom-call | tf_op jit(solution)/shard_map/radar/pallas_call | solution.py:461
  44.8 1.5 %copy.6 = f32[4,2,8,256]{3,2,1,0:T(8,128)} copy(f32[4,2,8,256]{3,2,1,0:T(8,128)} %radar.1) | data formatting | bytes 131072

commit v6 on v5

--- a/solution.py
+++ b/solution.py
@@ -199,8 +199,15 @@
         device_id={"tm": right}, device_id_type=MESH)
     halo_copy.start()
 
+    halves = 2
+    steps = chips // halves
+    far_first = sorted(
+        ((a, b) for a in range(halves) for b in range(steps) if a or b),
+        key=lambda ab: -(2 * ab[0] + min(ab[1], steps - ab[1])))
+
     def chip_peer(j):
-        return lax.rem(chip + 1 + j, chips)
+        a, b = far_first[j]
+        return lax.rem(chip // steps + a, halves) * steps + lax.rem(chip % steps + b, steps)
 
     def core_copy(j):
         return pltpu.make_async_remote_copy(
@@ -216,8 +223,9 @@
         core_copy(chip_peer(j)).start()
         return 0
 
-    for j in range(chips):
+    for j in range(chips - 1):
         core_start(j, 0)
+    core_copy(chip).start()
 
     def rs_start(j, _):
         peer = chip_peer(j)
@@ -229,6 +237,9 @@
     reach_wait(0)
     reach_signal(1)
 
+    for j in range(chips - 1):
+        rs_start(j, 0)
+
     halo_copy.wait()
     ref = ref_ref[...]
     before = jnp.where(d == 0, 0.0, halo[...])
@@ -243,8 +254,6 @@
     for order, term in enumerate((taps_lo, taps_hi, taps_mid)):
         lag_tab[2 * TAPS * order : 2 * TAPS * (order + 1)] = term.astype(jnp.bfloat16)
 
-    for j in range(chips - 1):
-        rs_start(j, 0)
     reach_wait(1)
     reach_signal(2)
     core_copy(chip).wait_recv()
@@ -397,7 +406,8 @@
         core_copy(j).wait_send()
         return 0
 
-    lax.fori_loop(0, chips - 1, rs_drain, 0)
+    for j in range(chips - 1):
+        rs_drain(j, 0)
     lax.fori_loop(0, chips, core_drain, 0)
     lg_all.wait_recv()
 

time: 46.4 us -> 44.4 us (0.957); the launches traced: 46.3 us -> 43.7 us
  Pallas kernels: 44.8 us -> 42.2 us
    pallas_call x1, Pallas kernels: 44.8 us -> 42.2 us  [on_device(): pl.pallas_call(functools.partial(kernel, nc, nt), out_shape=jax.ShapeDtyp...]
where the time goes in v6:
time: 44.4 us; the launch traced here: 43.7 us
  Pallas kernels  42.2 us (95%)
  local copies, waits for them, and re-layouts  1.47 us (3%)
    pallas_call x1, Pallas kernels, on_device(): pl.pallas_call(functools.partial(kernel, nc, nt), out_shape=jax.ShapeDtyp...  42.2 us
    unnamed x1, local copies, waits for them, and re-layouts  1.47 us

profile of v6, /device:TPU:6, one launch (start us, length us, event | category | flops | bytes accessed | tf_op | source)
XLA Modules:
  0.0 43.7 jit_solution(4340865525508536889)
XLA Ops:
  0.0 42.2 %radar.1 = f32[4,2,8,256]{3,2,1,0:T(8,128)} custom-call(f32[2,2048]{1,0:T(2,128)} %ref_hbm.1, f32[2,16,2048]{2,1,0:T(8,128)} %surv_hbm.1, f32[2,16,64]{2,1,0:T(8,128)} %bitcast.1, bf16[2,512,512]{2,1,0:T(8,128)(2,1)} %constant.2.clone.table_hbm), custom_call_target="tpu_custom_call" | custom-call | tf_op jit(solution)/shard_map/radar/pallas_call | solution.py:471
  42.2 1.5 %copy.6 = f32[4,2,8,256]{3,2,1,0:T(8,128)} copy(f32[4,2,8,256]{3,2,1,0:T(8,128)} %radar.1) | data formatting | bytes 131072

commit v7 on v6

--- a/solution.py
+++ b/solution.py
@@ -308,6 +308,21 @@
     tm_start(gm_copy)
     gm_buf[d] = gm[...]
 
+    def rs_wait(j, _):
+        peer = chip_peer(j)
+        rs_copy(peer, peer).wait_recv()
+        return 0
+
+    total = chip_buf[chip]
+    for j in reversed(range(chips - 1)):
+        rs_wait(j, 0)
+        total = total + chip_buf[chip_peer(j)]
+
+    x_raw = lag_products(total)
+    xm[...] = conj_pack(x_raw[:beams], x_raw[beams:])
+    tm_start(xm_copy)
+    xm_buf[d] = xm[...]
+
     for p in range(2):
         hi, mid = split(lags_of(p, TAPS, LAGS - TAPS), 2)
         for group in range(1, LAGS // TAPS):
@@ -315,22 +330,6 @@
             base = 2 * TAPS + 4 * TAPS * group + TAPS * p
             lag_tab[base : base + TAPS] = hi[rows].astype(jnp.bfloat16)
             lag_tab[base + 2 * TAPS : base + 3 * TAPS] = mid[rows].astype(jnp.bfloat16)
-
-    def rs_wait(j, _):
-        peer = chip_peer(j)
-        rs_copy(peer, peer).wait_recv()
-        return 0
-
-    for j in range(chips - 1):
-        rs_wait(j, 0)
-    total = chip_buf[0]
-    for source in range(1, chips):
-        total = total + chip_buf[source]
-
-    x_raw = lag_products(total)
-    xm[...] = conj_pack(x_raw[:beams], x_raw[beams:])
-    tm_start(xm_copy)
-    xm_buf[d] = xm[...]
 
     gm_all.wait_recv()
     g_sum = jnp.sum(gm_buf[...], axis=0)

time: 44.4 us -> 44.4 us (level)
  no operation moved by 1% of the time
where the time goes in v7:
time: 44.4 us; the launch traced here: 43.7 us
  Pallas kernels  42.2 us (95%)
  local copies, waits for them, and re-layouts  1.47 us (3%)
    pallas_call x1, Pallas kernels, on_device(): pl.pallas_call(functools.partial(kernel, nc, nt), out_shape=jax.ShapeDtyp...  42.2 us
    unnamed x1, local copies, waits for them, and re-layouts  1.47 us

profile of v7, /device:TPU:6, one launch (start us, length us, event | category | flops | bytes accessed | tf_op | source)
XLA Modules:
  0.0 43.7 jit_solution(655296727265685376)
XLA Ops:
  0.0 42.2 %radar.1 = f32[4,2,8,256]{3,2,1,0:T(8,128)} custom-call(f32[2,2048]{1,0:T(2,128)} %ref_hbm.1, f32[2,16,2048]{2,1,0:T(8,128)} %surv_hbm.1, f32[2,16,64]{2,1,0:T(8,128)} %bitcast.1, bf16[2,512,512]{2,1,0:T(8,128)(2,1)} %constant.2.clone.table_hbm), custom_call_target="tpu_custom_call" | custom-call | tf_op jit(solution)/shard_map/radar/pallas_call | solution.py:470
  42.2 1.5 %copy.6 = f32[4,2,8,256]{3,2,1,0:T(8,128)} copy(f32[4,2,8,256]{3,2,1,0:T(8,128)} %radar.1) | data formatting | bytes 131072
